TPU v7x, 256 devices: a whole 4x4x8 slice. The times are simulated.
256 devices in a mesh: pix: 64 (over x, z, core), band: 4 (over y).
Axes of the slice: x: 4, y: 4, z: 8, core: 2. Of those that a mesh axis runs over, the one named last changes fastest.
Arguments:
- spectra: bfloat16 [224, 262144], P('band', 'pix'), may hold values from -0.1 to 4
- endmembers: bfloat16 [224, 512], P('band'), may hold values from 0.05 to 1
- gram_inverse: float32 [512, 512], replicated, may hold values from -1 to 1, as said below
- abundances: float32 [512, 262144], P(None, ('pix', 'band')), may hold values from 0 to 512, as said below
- duals: float32 [512, 262144], P(None, ('pix', 'band')), may hold values from -4 to 4
Outputs:
- abundances_out: float32 [512, 262144], P(None, ('pix', 'band'))
- duals_out: float32 [512, 262144], P(None, ('pix', 'band'))
- residual_rms: float32 [2, 2], replicated
Inputs may be any that keep to these rules, and one draw needn't show every extreme that they name: `abundances`: each column is nonnegative and sums to 512. `gram_inverse`: penalty times the float32 inverse of endmembers^T endmembers / 512^2 + penalty I, with penalty = 224 / (2 * 512^2) and the endmembers as stored.
All inputs are finite; a program needn't handle non-finite values.
Results may differ from a plain program's by a relative error of at most 0.0004.
Values may be sent and summed in bfloat16 or wider, within the bound.
A program may use at most 64 MiB of HBM per device.

v0:
```python
import jax
import jax.numpy as jnp
from jax import lax
from jax.sharding import Mesh
from jax.sharding import PartitionSpec as P

B = 224
K = 512
ITERS = 2
BISECT = 6
PIX = ("pix_0", "pix_1", "pix_2")
PIX_BAND = ("pix_0", "pix_1", "pix_2", "band")


def one_axis_at_a_time(shard, axes):
    for axis in axes:
        shard = lax.psum(shard, axis)
    return shard


def project(shifted):
    simplex_sum = float(K)
    high_end = jnp.max(shifted, axis=0)
    low_end = (jnp.sum(shifted, axis=0) - simplex_sum) / simplex_sum

    def mass_at(level):
        return jnp.sum(jnp.maximum(shifted - level[None, :], 0.0), axis=0)

    mass_low = mass_at(low_end)
    mass_high = jnp.zeros_like(high_end)

    def bisect_once(unused, state):
        low_now, high_now, low_mass, high_mass = state
        middle = 0.5 * (low_now + high_now)
        total_mass = mass_at(middle)
        too_high = total_mass > simplex_sum
        return (
            jnp.where(too_high, middle, low_now),
            jnp.where(too_high, high_now, middle),
            jnp.where(too_high, total_mass, low_mass),
            jnp.where(too_high, high_mass, total_mass),
        )

    low_end, high_end, mass_low, mass_high = lax.fori_loop(
        0, BISECT, bisect_once, (low_end, high_end, mass_low, mass_high)
    )
    level = low_end + (mass_low - simplex_sum) * (high_end - low_end) / (mass_low - mass_high)
    return jnp.maximum(shifted - level[None, :], 0.0)


def contract_bands(signatures, columns):
    return lax.dot_general(
        signatures, columns, (((0,), (0,)), ((), ())), preferred_element_type=jnp.float32
    )


def body(spectra, endmembers, gram_inverse, abundances, duals):
    penalty = B / (2.0 * K * K)
    exchanged = lax.all_to_all(spectra, "band", split_axis=1, concat_axis=0, tiled=True)
    all_rows = lax.all_gather(endmembers, "band", axis=0, tiled=True)
    fit_term = contract_bands(all_rows, exchanged)
    fit_term = fit_term / K
    pixel_count = abundances.shape[1] * lax.axis_size(PIX) * lax.axis_size("band")
    current = abundances
    scaled_dual = duals
    primal_list = []
    change_list = []
    for sweep in range(ITERS):
        primal = jnp.dot(
            gram_inverse,
            fit_term / penalty + current - scaled_dual,
            precision=lax.Precision.HIGHEST,
        )
        updated = project(primal + scaled_dual)
        scaled_dual = scaled_dual + primal - updated
        primal_sum = jnp.sum((primal - updated) ** 2)
        change_sum = jnp.sum((updated - current) ** 2)
        primal_list.append(primal_sum)
        change_list.append(change_sum)
        current = updated
    totals = jnp.stack([jnp.stack(primal_list), jnp.stack(change_list)])
    totals = one_axis_at_a_time(totals, PIX_BAND)
    residual_rms = jnp.sqrt(totals / pixel_count)
    return (current, scaled_dual, residual_rms)


def solution(mesh):
    finer = Mesh(
        mesh.devices.reshape(4, 8, 2, mesh.shape["band"]), ("pix_0", "pix_1", "pix_2", "band")
    )
    return jax.shard_map(
        body,
        mesh=finer,
        in_specs=(P("band", PIX), P("band", None), P(), P(None, PIX_BAND), P(None, PIX_BAND)),
        out_specs=(P(None, PIX_BAND), P(None, PIX_BAND), P()),
        check_vma=False,
    )
```

profile of v0, /device:TPU:1, one launch (start us, length us, event | category | flops | bytes accessed | tf_op | source)
XLA Modules:
  0.0 109.2 jit_solution(441457199507730125)
XLA Ops:
  0.6 0.0 copy-start
  0.6 1.9 %copy.12 = bf16[7,4,8,1024]{3,2,0,1:T(8,128)(2,1)} copy(bf16[7,4,8,1024]{3,2,1,0:T(8,128)(2,1)} %bitcast.36) | data formatting | bytes 917504 | tf_op jit(solution)/shard_map/all_to_all | solution.py:59
  2.5 5.0 %all-to-all-start = ((bf16[56,4,1024]{2,0,1:T(8,128)(2,1)}), bf16[56,4,1024]{2,0,1:T(8,128)(2,1)S(1)}, u32[]{:S(2)}, u32[]{:S(2)}) async-start(bf16[56,4,1024]{2,0,1:T(8,128)(2,1)} %bitcast.34), calls=%async_computation | async-start | bytes 917504 | tf_op jit(solution)/shard_map/all_to_all | solution.py:59
  7.6 12.5 %all_gather.3 = bf16[224,512]{1,0:T(8,128)(2,1)S(1)} all-gather(bf16[56,512]{1,0:T(8,128)(2,1)} %param.10), channel_id=1, replica_groups=mesh['pix_0'=4,'pix_1'=8,'pix_2'=2,'band'=4] {'band'}, dimensions={0}, use_global_device_ids=true | all-gather | bytes 286720 | tf_op jit(solution)/shard_map/all_gather | solution.py:60
  20.0 0.0 all-to-all-done
  20.0 0.5 fusion.29
  20.5 0.0 copy-done
  20.5 0.0 copy-start.2
  20.5 8.7 %fusion.28 = (f32[1024]{0:T(1024)S(1)}, f32[512,1024]{1,0:T(8,128)S(1)}, f32[1024,512]{0,1:T(8,128)}) fusion(f32[512,1024]{1,0:T(8,128)} %param.13, f32[512,512]{1,0:T(8,128)S(1)} %copy-done, f32[512,1024]{1,0:T(8,128)} %param.12, f32[512,1024]{1,0:T(8,128)S(1)} %fusion.29), kind=kOutput, calls=%fused_computation.54 | convolution fusion | flops 3223845888 | bytes 11538432 | tf_op jit(solution)/shard_map/dot_general | solution.py:69
  29.2 0.0 copy-done.2
  29.2 0.3 maximum_reduce_fusion.3
  29.5 1.9 %while.34 = (s32[]{:T(128)}, f32[1024]{0:T(1024)S(1)}, f32[1024]{0:T(1024)S(1)}, f32[1024]{0:T(1024)S(1)}, f32[1024]{0:T(1024)S(1)}, /*index=5*/f32[512,1024]{1,0:T(8,128)S(1)}, s32[]{:T(128)}, s32[]{:T(128)}) while((s32[]{:T(128)}, f32[1024]{0:T(1024)S(1)}, f32[1024]{0:T(1024)S(1)}, f32[1024]{0:T(1024)S(1)}, f32[1024]{0:T(1024)S(1)}, ...), condition=%wide.region_5.6_spmd.clone, body=%wide.region_3.5_spmd.clone.sunk | while | flops 1582083 | bytes 2154591 | solution.py:44
  29.6 0.3 maximum_reduce_fusion.6
  29.9 0.3 maximum_reduce_fusion.6
  30.2 0.3 maximum_reduce_fusion.6
  30.5 0.3 maximum_reduce_fusion.6
  30.8 0.3 maximum_reduce_fusion.6
  31.2 0.3 maximum_reduce_fusion.6
  31.5 7.0 %fusion.27 = (f32[1024]{0:T(1024)S(1)}, f32[512,1024]{1,0:T(8,128)S(1)}, f32[1024,512]{0,1:T(8,128)}) fusion(f32[512,1024]{1,0:T(8,128)S(1)} %get-tuple-element.310, f32[1024]{0:T(1024)S(1)} %divide_add_fusion.1, f32[512,512]{1,0:T(8,128)S(1)} %copy-done, f32[512,1024]{1,0:T(8,128)} %copy-done.2), kind=kOutput, calls=%fused_computation.53 | convolution fusion | flops 3226991616 | bytes 9445376 | tf_op jit(solution)/shard_map/dot_general | solution.py:69
  38.5 0.0 copy-start.1
  38.5 0.3 maximum_reduce_fusion.2
  38.8 1.0 copy-done.1
  39.8 11.3 %while.35 = (s32[]{:T(128)}, f32[1024]{0:T(1024)S(1)}, f32[1024]{0:T(1024)S(1)}, f32[1024]{0:T(1024)S(1)}, f32[1024]{0:T(1024)S(1)}, /*index=5*/f32[512,1024]{1,0:T(8,128)}, s32[]{:T(128)}, s32[]{:T(128)}) while((s32[]{:T(128)}, f32[1024]{0:T(1024)S(1)}, f32[1024]{0:T(1024)S(1)}, f32[1024]{0:T(1024)S(1)}, f32[1024]{0:T(1024)S(1)}, ...), condition=%wide.region_11.12_spmd.clone, body=%wide.region_9.0_spmd.clone.sunk | while | flops 1582083 | bytes 2154591 | solution.py:44
  39.8 1.8 %maximum_reduce_fusion.7 = f32[1024]{0:T(1024)S(1)} fusion(f32[512,1024]{1,0:T(8,128)} %get-tuple-element.307, f32[1024]{0:T(1024)S(1)} %add_multiply_fusion.7), kind=kLoop, calls=%fused_computation.7.clone.1 | loop fusion | flops 1571840 | bytes 2105344 | tf_op jit(solution)/shard_map/while/body/eval_jaxpr/reduce_sum | solution.py:27
  41.7 1.8 %maximum_reduce_fusion.7 = f32[1024]{0:T(1024)S(1)} fusion(f32[512,1024]{1,0:T(8,128)} %get-tuple-element.307, f32[1024]{0:T(1024)S(1)} %add_multiply_fusion.7), kind=kLoop, calls=%fused_computation.7.clone.1 | loop fusion | flops 1571840 | bytes 2105344 | tf_op jit(solution)/shard_map/while/body/eval_jaxpr/reduce_sum | solution.py:27
  43.6 1.8 %maximum_reduce_fusion.7 = f32[1024]{0:T(1024)S(1)} fusion(f32[512,1024]{1,0:T(8,128)} %get-tuple-element.307, f32[1024]{0:T(1024)S(1)} %add_multiply_fusion.7), kind=kLoop, calls=%fused_computation.7.clone.1 | loop fusion | flops 1571840 | bytes 2105344 | tf_op jit(solution)/shard_map/while/body/eval_jaxpr/reduce_sum | solution.py:27
  45.5 1.8 %maximum_reduce_fusion.7 = f32[1024]{0:T(1024)S(1)} fusion(f32[512,1024]{1,0:T(8,128)} %get-tuple-element.307, f32[1024]{0:T(1024)S(1)} %add_multiply_fusion.7), kind=kLoop, calls=%fused_computation.7.clone.1 | loop fusion | flops 1571840 | bytes 2105344 | tf_op jit(solution)/shard_map/while/body/eval_jaxpr/reduce_sum | solution.py:27
  47.3 1.8 %maximum_reduce_fusion.7 = f32[1024]{0:T(1024)S(1)} fusion(f32[512,1024]{1,0:T(8,128)} %get-tuple-element.307, f32[1024]{0:T(1024)S(1)} %add_multiply_fusion.7), kind=kLoop, calls=%fused_computation.7.clone.1 | loop fusion | flops 1571840 | bytes 2105344 | tf_op jit(solution)/shard_map/while/body/eval_jaxpr/reduce_sum | solution.py:27
  49.2 1.8 %maximum_reduce_fusion.7 = f32[1024]{0:T(1024)S(1)} fusion(f32[512,1024]{1,0:T(8,128)} %get-tuple-element.307, f32[1024]{0:T(1024)S(1)} %add_multiply_fusion.7), kind=kLoop, calls=%fused_computation.7.clone.1 | loop fusion | flops 1571840 | bytes 2105344 | tf_op jit(solution)/shard_map/while/body/eval_jaxpr/reduce_sum | solution.py:27
  51.1 7.0 %fusion.9 = (f32[]{:T(128)}, f32[]{:T(128)}, f32[]{:T(128)}, f32[]{:T(128)}, f32[512,1024]{1,0:T(8,128)}) fusion(f32[1024,512]{0,1:T(8,128)} %get-tuple-element.168, f32[512,1024]{1,0:T(8,128)S(1)} %get-tuple-element.310, f32[1024]{0:T(1024)S(1)} %divide_add_fusion.1, f32[512,1024]{1,0:T(8,128)} %param.12, f32[1024,512]{0,1:T(8,128)} %get-tuple-element.169, ...), kind=kLoop, calls=%fused_computation.21 | loop fusion | flops 8388604 | bytes 12591120 | tf_op jit(solution)/shard_map/reduce_sum | solution.py:76
  58.1 2.6 %maximum_bitcast_fusion = (f32[1,2]{1,0:T(1,128)S(1)}, f32[1,2]{1,0:T(1,128)S(1)}) fusion(f32[1]{0:T(128)} %bitcast.5, f32[1]{0:T(128)} %bitcast.4, f32[1]{0:T(128)} %bitcast.8, f32[1]{0:T(128)} %bitcast.7), kind=kLoop, calls=%fused_computation.48 | loop fusion | flops 4 | bytes 32 | tf_op jit(solution)/shard_map/stack | solution.py:81
  60.7 8.0 %psum.28 = f32[2,2]{1,0:T(2,128)S(1)} all-reduce(f32[2,2]{1,0:T(2,128)S(1)} %pad_maximum_fusion), channel_id=1, replica_groups=mesh['pix_0'=4,'pix_1'=8,'pix_2'=2,'band'=4] {'pix_0'}, use_global_device_ids=true, to_apply=%region_16.17 | all-reduce | flops 4 | bytes 32 | tf_op jit(solution)/shard_map/psum | solution.py:17
  68.8 16.2 %psum.29 = f32[2,2]{1,0:T(2,128)S(1)} all-reduce(f32[2,2]{1,0:T(2,128)S(1)} %psum.28), channel_id=1, replica_groups=mesh['pix_0'=4,'pix_1'=8,'pix_2'=2,'band'=4] {'pix_1'}, use_global_device_ids=true, to_apply=%region_17.18 | all-reduce | flops 4 | bytes 32 | tf_op jit(solution)/shard_map/psum | solution.py:17
  85.0 12.4 %psum.30 = f32[2,2]{1,0:T(2,128)S(1)} all-reduce(f32[2,2]{1,0:T(2,128)S(1)} %psum.29), channel_id=1, replica_groups=mesh['pix_0'=4,'pix_1'=8,'pix_2'=2,'band'=4] {'pix_2'}, use_global_device_ids=true, to_apply=%region_18.19 | all-reduce | flops 4 | bytes 32 | tf_op jit(solution)/shard_map/psum | solution.py:17
  97.4 7.1 %psum.31 = f32[2,2]{1,0:T(2,128)S(1)} all-reduce(f32[2,2]{1,0:T(2,128)S(1)} %psum.30), channel_id=1, replica_groups=mesh['pix_0'=4,'pix_1'=8,'pix_2'=2,'band'=4] {'band'}, use_global_device_ids=true, to_apply=%region_19.20 | all-reduce | flops 4 | bytes 32 | tf_op jit(solution)/shard_map/psum | solution.py:17
  104.5 0.6 multiply_sqrt_fusion
  105.1 4.1 %sub.115 = f32[512,1024]{1,0:T(8,128)} subtract(f32[512,1024]{1,0:T(8,128)} %get-tuple-element.311, f32[512,1024]{1,0:T(8,128)} %get-tuple-element.155) | non-fusion elementwise | flops 524288 | bytes 6291456 | tf_op jit(solution)/shard_map/sub | solution.py:75
  (31 shorter events, 0.2 us)
Async XLA Ops:
  0.6 19.9 %copy-start = (f32[512,512]{1,0:T(8,128)S(1)}, f32[512,512]{1,0:T(8,128)}, u32[]{:S(2)}) copy-start(f32[512,512]{1,0:T(8,128)} %param.11) | copy-start | bytes 3145732
  2.5 17.5 %all-to-all-start = ((bf16[56,4,1024]{2,0,1:T(8,128)(2,1)}), bf16[56,4,1024]{2,0,1:T(8,128)(2,1)S(1)}, u32[]{:S(2)}, u32[]{:S(2)}) async-start(bf16[56,4,1024]{2,0,1:T(8,128)(2,1)} %bitcast.34), calls=%async_computation | async-start | bytes 917504 | tf_op jit(solution)/shard_map/all_to_all | solution.py:59
  20.5 8.7 %copy-start.2 = (f32[512,1024]{1,0:T(8,128)}, f32[512,1024]{1,0:T(8,128)S(1)}, u32[]{:S(2)}) copy-start(f32[512,1024]{1,0:T(8,128)S(1)} %fusion.29) | copy-start | bytes 6291460
  38.5 1.4 %copy-start.1 = (f32[512,1024]{1,0:T(8,128)}, f32[512,1024]{1,0:T(8,128)S(1)}, u32[]{:S(2)}) copy-start(f32[512,1024]{1,0:T(8,128)S(1)} %get-tuple-element.291) | copy-start | bytes 6291460
where the time goes:
time: 110 us; the launch traced here: 109 us
  blocking collectives  56.2 us (51%)
  other arithmetic  27.9 us (25%)
  matrix products  16.1 us (15%)
  starting transfers between devices  5 us (5%)
  local copies, waits for them, and re-layouts  2.93 us (3%)
    psum x4, blocking collectives, one_axis_at_a_time(): shard = lax.psum(shard, axis)  43.7 us
    dot_general x2, matrix products, body(): jnp.dot(gram_inverse, fit_term / penalty + current - scaled_dual, precisi...  15.7 us
    reduce_sum x14, other arithmetic, mass_at(): return jnp.sum(jnp.maximum(shifted - level[None, :], 0.0), axis=0)  13.3 us
    all_gather x1, blocking collectives, body(): all_rows = lax.all_gather(endmembers, 'band', axis=0, tiled=True)  12.5 us
    reduce_sum x1, other arithmetic, body(): primal_sum = jnp.sum((primal - updated) ** 2)  7.01 us
    all_to_all x1, starting transfers between devices, body(): lax.all_to_all(spectra, 'band', split_axis=1, concat_axis=0, tiled=True)  5 us
    sub x1, other arithmetic, body(): scaled_dual = scaled_dual + primal - updated  4.1 us
    another operation x2, other arithmetic, body(): totals = jnp.stack([jnp.stack(primal_list), jnp.stack(change_list)])  2.64 us
  transfers between devices with their start and end apart: 1, of which 0 were waited for; matrix products, arithmetic and copies ran while one was open for 0% of the time, Pallas kernels for 0%

commit v1 on v0

v1 whole, which is shorter than its diff:
```python
import functools

import jax
import jax.numpy as jnp
from jax import lax
from jax.experimental import pallas as pl
from jax.experimental.pallas import tpu as pltpu
from jax.sharding import PartitionSpec as P

K = 512
BISECT = 6
MESH = pl.DeviceIdType.MESH
F32 = jnp.float32
BF16 = jnp.bfloat16
CHUNK = 256


def mxu(a, b):
    return jnp.dot(a, b, preferred_element_type=F32)


def split(value):
    high = value.astype(BF16)
    return high, (value - high.astype(F32)).astype(BF16)


def gather_kernel(bands, padded, scale, spectra, endmembers, gram, y_out, e_out, m_high, m_low,
                  e_send, e_recv, y_send, y_recv, own_sem):
    me = lax.axis_index("band")
    rows = spectra.shape[0]
    columns = y_out.shape[1]
    mine = pl.ds(pl.multiple_of(me * padded, padded), rows)

    own_e = pltpu.make_async_copy(endmembers, e_out.at[mine, :], own_sem.at[0])
    own_y = pltpu.make_async_copy(
        spectra.at[:, pl.ds(pl.multiple_of(me * columns, columns), columns)],
        y_out.at[mine, :], own_sem.at[1])
    barrier = pltpu.get_barrier_semaphore()
    for step in range(1, bands):
        pl.semaphore_signal(barrier, inc=1, device_id={"band": lax.rem(me + step, bands)},
                            device_id_type=MESH)
    if padded > rows:
        for band in range(bands):
            start = band * padded + rows
            y_out[start:start + padded - rows, :] = jnp.zeros((padded - rows, columns), BF16)
            e_out[start:start + padded - rows, :] = jnp.zeros((padded - rows, K), BF16)
    own_e.start()
    own_y.start()
    pl.semaphore_wait(barrier, bands - 1)

    copies_e, copies_y = [], []
    for step in range(1, bands):
        peer = lax.rem(me + step, bands)
        copies_e.append(pltpu.make_async_remote_copy(
            src_ref=endmembers, dst_ref=e_out.at[mine, :],
            send_sem=e_send.at[step - 1], recv_sem=e_recv.at[step - 1],
            device_id={"band": peer}, device_id_type=MESH))
        copies_e[-1].start()
    for step in range(1, bands):
        peer = lax.rem(me + step, bands)
        copies_y.append(pltpu.make_async_remote_copy(
            src_ref=spectra.at[:, pl.ds(pl.multiple_of(peer * columns, columns), columns)],
            dst_ref=y_out.at[mine, :],
            send_sem=y_send.at[step - 1], recv_sem=y_recv.at[step - 1],
            device_id={"band": peer}, device_id_type=MESH))
        copies_y[-1].start()
    own_e.wait()
    for copy in copies_e:
        copy.wait_recv()
    signatures = e_out[...]
    total = jnp.zeros((K, bands * padded), F32)
    rest = gram[...]
    for _ in range(3):
        high = rest.astype(BF16)
        total += lax.dot_general(high, signatures, (((1,), (1,)), ((), ())), preferred_element_type=F32)
        rest = rest - high.astype(F32)
    high, low = split(total * scale)
    m_high[...] = high
    m_low[...] = low
    own_y.wait()
    for copy in copies_y:
        copy.wait_recv()
    for copy in copies_e + copies_y:
        copy.wait_send()


def mass(shifted, level):
    return jnp.sum(jnp.maximum(shifted, level), axis=0, keepdims=True) - K * level


def find_level(shifted):
    high = jnp.max(shifted, axis=0, keepdims=True)
    low = (jnp.sum(shifted, axis=0, keepdims=True) - K) / K
    mass_low = mass(shifted, low)
    mass_high = jnp.zeros_like(high)
    for _ in range(BISECT):
        middle = 0.5 * (low + high)
        total = mass(shifted, middle)
        above = total > K
        low = jnp.where(above, middle, low)
        high = jnp.where(above, high, middle)
        mass_low = jnp.where(above, total, mass_low)
        mass_high = jnp.where(above, mass_high, total)
    return low + (mass_low - K) * (high - low) / (mass_low - mass_high)


def admm_kernel(y_ref, e_ref, mh_ref, ml_ref, z_ref, u_ref, z_out, u_out, sums):
    step = pl.program_id(0)
    current, dual = z_ref[...], u_ref[...]
    spectra = y_ref[...].astype(F32)
    signatures, m_high, m_low = e_ref[...], mh_ref[...], ml_ref[...]
    parts = []
    for sweep in range(2):
        high, low = split(current - dual)
        rest = spectra - (mxu(signatures, high) + mxu(signatures, low)) * (1.0 / K)
        high, low = split(rest)
        shifted = current + (mxu(m_high, high) + mxu(m_low, high) + mxu(m_high, low))
        level = find_level(shifted)
        updated = jnp.maximum(shifted - level, 0.0)
        new_dual = jnp.minimum(shifted, level)
        parts.append(jnp.sum((new_dual - dual) ** 2, axis=0, keepdims=True))
        parts.append(jnp.sum((updated - current) ** 2, axis=0, keepdims=True))
        current, dual = updated, new_dual
    z_out[...] = current
    u_out[...] = dual

    @pl.when(step == 0)
    def _():
        sums[...] = jnp.zeros_like(sums)
    lane = lax.broadcasted_iota(jnp.int32, (1, 128), 1)
    row = jnp.zeros((1, 128), F32)
    for place, part in enumerate((parts[0], parts[2], parts[1], parts[3])):
        row = row + jnp.where(lane == place, jnp.sum(part, axis=1, keepdims=True), 0.0)
    sums[...] += row


def reduce_kernel(bands, sums, out, first, second, mid, send1, recv1, send2, recv2):
    pix, band = lax.axis_index("pix"), lax.axis_index("band")
    inner, outer = 16, 4
    low, x = lax.rem(pix, inner), pix // inner
    place = x * bands + band
    barrier = pltpu.get_barrier_semaphore()

    def target1(step):
        return {"pix": x * inner + lax.rem(low + step, inner), "band": band}

    def target2(step):
        other = lax.rem(place + step, outer * bands)
        return {"pix": (other // bands) * inner + low, "band": lax.rem(other, bands)}

    for step in range(1, inner):
        pl.semaphore_signal(barrier, inc=1, device_id=target1(step), device_id_type=MESH)
    for step in range(1, outer * bands):
        pl.semaphore_signal(barrier, inc=1, device_id=target2(step), device_id_type=MESH)
    first[0] = sums[...]
    pl.semaphore_wait(barrier, inner - 1 + outer * bands - 1)
    copies1, copies2 = [], []
    for step in range(1, inner):
        copies1.append(pltpu.make_async_remote_copy(
            src_ref=sums, dst_ref=first.at[step], send_sem=send1.at[step], recv_sem=recv1.at[step],
            device_id=target1(step), device_id_type=MESH))
        copies1[-1].start()
    for copy in copies1:
        copy.wait_recv()
    total = jnp.sum(first[...], axis=0)
    mid[...] = total
    second[0] = total
    for step in range(1, outer * bands):
        copies2.append(pltpu.make_async_remote_copy(
            src_ref=mid, dst_ref=second.at[step], send_sem=send2.at[step], recv_sem=recv2.at[step],
            device_id=target2(step), device_id_type=MESH))
        copies2[-1].start()
    for copy in copies2:
        copy.wait_recv()
    out[...] = jnp.sum(second[...], axis=0)
    for copy in copies1 + copies2:
        copy.wait_send()


def body(bands, pixels, total_bands, spectra, endmembers, gram_inverse, abundances, duals):
    rows = spectra.shape[0]
    padded = -(-rows // 64) * 64
    depth = bands * padded
    columns = abundances.shape[1]
    penalty = total_bands / (2.0 * K * K)
    vmem = pl.BlockSpec(memory_space=pltpu.VMEM)
    anywhere = pl.BlockSpec(memory_space=pl.ANY)
    y, e, m_high, m_low = pl.pallas_call(
        functools.partial(gather_kernel, bands, padded, 1.0 / (K * penalty)),
        out_shape=(jax.ShapeDtypeStruct((depth, columns), BF16), jax.ShapeDtypeStruct((depth, K), BF16),
                   jax.ShapeDtypeStruct((K, depth), BF16), jax.ShapeDtypeStruct((K, depth), BF16)),
        in_specs=[anywhere, anywhere, vmem],
        out_specs=(vmem,) * 4,
        scratch_shapes=[pltpu.SemaphoreType.DMA((bands - 1,))] * 4 + [pltpu.SemaphoreType.DMA((2,))],
        compiler_params=pltpu.CompilerParams(collective_id=0, has_side_effects=True),
        name="gather",
    )(spectra, endmembers, gram_inverse)
    whole = lambda i: (0, 0)
    block = lambda i: (0, i)
    z, u, sums = pl.pallas_call(
        admm_kernel,
        grid=(columns // CHUNK,),
        out_shape=(jax.ShapeDtypeStruct((K, columns), F32), jax.ShapeDtypeStruct((K, columns), F32),
                   jax.ShapeDtypeStruct((1, 128), F32)),
        in_specs=[pl.BlockSpec((depth, CHUNK), block), pl.BlockSpec((depth, K), whole),
                  pl.BlockSpec((K, depth), whole), pl.BlockSpec((K, depth), whole),
                  pl.BlockSpec((K, CHUNK), block), pl.BlockSpec((K, CHUNK), block)],
        out_specs=(pl.BlockSpec((K, CHUNK), block), pl.BlockSpec((K, CHUNK), block),
                   pl.BlockSpec((1, 128), whole)),
        name="admm",
    )(y, e, m_high, m_low, abundances, duals)
    n1, n2 = 16, 4 * bands
    totals = pl.pallas_call(
        functools.partial(reduce_kernel, bands),
        out_shape=jax.ShapeDtypeStruct((1, 128), F32),
        in_specs=[vmem],
        out_specs=vmem,
        scratch_shapes=[pltpu.VMEM((n1, 1, 128), F32), pltpu.VMEM((n2, 1, 128), F32), pltpu.VMEM((1, 128), F32),
                        pltpu.SemaphoreType.DMA((n1,)), pltpu.SemaphoreType.DMA((n1,)),
                        pltpu.SemaphoreType.DMA((n2,)), pltpu.SemaphoreType.DMA((n2,))],
        compiler_params=pltpu.CompilerParams(collective_id=1, has_side_effects=True),
        name="reduce",
    )(sums)
    residual_rms = jnp.sqrt(totals[0, :4].reshape(2, 2) / pixels)
    return z, u, residual_rms


def solution(mesh):
    bands = mesh.shape["band"]

    def run(spectra, endmembers, gram_inverse, abundances, duals):
        step = functools.partial(body, bands, abundances.shape[1], spectra.shape[0])
        return jax.shard_map(
            step,
            mesh=mesh,
            in_specs=(P("band", "pix"), P("band", None), P(), P(None, ("pix", "band")), P(None, ("pix", "band"))),
            out_specs=(P(None, ("pix", "band")), P(None, ("pix", "band")), P()),
            check_vma=False,
        )(spectra, endmembers, gram_inverse, abundances, duals)

    return run
```

time: 110 us -> 52.1 us (0.47)
  blocking collectives: 56.2 us -> 0 us
  Pallas kernels: 0 us -> 50 us
  other arithmetic: 27.9 us -> 0.7 us
  matrix products: 16.1 us -> 0 us
  starting transfers between devices: 5 us -> 0 us
  local copies, waits for them, and re-layouts: 2.93 us -> 0.65 us
    pallas_call x0 -> x3, Pallas kernels: none -> 50 us  [the longest x1 19.7 us: body(): pl.pallas_call(functools.partial(reduce_kernel, bands), out_shape=jax.Sha...]
    psum x4 -> x0, blocking collectives: 43.7 us -> none  [one_axis_at_a_time(): shard = lax.psum(shard, axis)]
    reduce_sum x15 -> x0, other arithmetic: 20.3 us -> none  [the longest x14 13.3 us: mass_at(): return jnp.sum(jnp.maximum(shifted - level[None, :], 0.0), axis=0)]
    dot_general x3 -> x0, matrix products: 16.1 us -> none  [the longest x2 15.7 us: body(): jnp.dot(gram_inverse, fit_term / penalty + current - scaled_dual, precisi...]
    all_gather x1 -> x0, blocking collectives: 12.5 us -> none  [body(): all_rows = lax.all_gather(endmembers, 'band', axis=0, tiled=True)]
    all_to_all x1 -> x0, starting transfers between devices: 5 us -> none  [body(): lax.all_to_all(spectra, 'band', split_axis=1, concat_axis=0, tiled=True)]
    sub x1 -> x0, other arithmetic: 4.1 us -> none  [body(): scaled_dual = scaled_dual + primal - updated]
    another operation x2 -> x0, other arithmetic: 2.64 us -> none  [body(): totals = jnp.stack([jnp.stack(primal_list), jnp.stack(change_list)])]
  transfers between devices with their start and end apart: 1 -> 0, of which waited for: 0 -> 0; matrix products, arithmetic and copies ran while one was open for 0% -> 0% of each run, Pallas kernels for 0% -> 0%
where the time goes in v1:
time: 52.1 us; the launch traced here: 52 us
  Pallas kernels  50 us (96%)
  other arithmetic  0.7 us (1%)
  local copies, waits for them, and re-layouts  0.65 us (1%)
  between operations  0.65 us (1%)
    pallas_call x1, Pallas kernels, body(): pl.pallas_call(functools.partial(reduce_kernel, bands), out_shape=jax.Sha...  19.7 us
    pallas_call x1, Pallas kernels, body(): pl.pallas_call(admm_kernel, grid=(columns // CHUNK,), out_shape=(jax.Shap...  15.9 us
    pallas_call x1, Pallas kernels, body(): pl.pallas_call(functools.partial(gather_kernel, bands, padded, 1.0 / (K *...  14.4 us

profile of v1, /device:TPU:1, one launch (start us, length us, event | category | flops | bytes accessed | tf_op | source)
XLA Modules:
  0.0 52.0 jit_solution(15692543427298072078)
XLA Ops:
  0.6 14.4 %gather.1 = (bf16[256,1024]{1,0:T(8,128)(2,1)}, bf16[256,512]{1,0:T(8,128)(2,1)}, bf16[512,256]{1,0:T(8,128)(2,1)}, bf16[512,256]{1,0:T(8,128)(2,1)}) custom-call(bf16[56,4096]{1,0:T(8,128)(2,1)} %spectra.1, bf16[56,512]{1,0:T(8,128)(2,1)} %endmembers.1, f32[512,512]{1,0:T(8,128)} %gram.1), custom_call_target="tpu_custom_call" | custom-call | tf_op jit(solution)/shard_map/gather/pallas_call | solution.py:188
  15.1 15.9 %admm.1 = (f32[512,1024]{1,0:T(8,128)}, f32[512,1024]{1,0:T(8,128)}, f32[1,128]{1,0:T(1,128)}) custom-call(bf16[256,1024]{1,0:T(8,128)(2,1)} %get-tuple-element.10.y_ref, bf16[256,512]{1,0:T(8,128)(2,1)} %get-tuple-element.11.e_ref, bf16[512,256]{1,0:T(8,128)(2,1)} %get-tuple-element.12.mh_ref, bf16[512,256]{1,0:T(8,128)(2,1)} %get-tuple-element.13.ml_ref, ...), custom_call_target="tpu_custom_call" | custom-call | tf_op jit(solution)/shard_map/admm/pallas_call | solution.py:200
  30.9 19.7 %reduce.5 = f32[1,128]{1,0:T(1,128)} custom-call(f32[1,128]{1,0:T(1,128)} %get-tuple-element.16.sums), custom_call_target="tpu_custom_call" | custom-call | tf_op jit(solution)/shard_map/reduce/pallas_call | solution.py:213
  50.6 0.7 %sqrt_reduce_fusion = f32[4]{0:T(128)S(1)} fusion(f32[1,128]{1,0:T(1,128)} %reduce.5), kind=kLoop, calls=%fused_computation | loop fusion | flops 4 | bytes 32 | tf_op jit(solution)/shard_map/sqrt | solution.py:224
  51.3 0.6 %sqrt.7 = f32[2,2]{1,0:T(2,128)} reshape(f32[4]{0:T(128)S(1)} %sqrt_reduce_fusion) | data formatting | bytes 32 | tf_op jit(solution)/shard_map/sqrt | solution.py:224

commit v2 on v0

v2 whole, which is shorter than its diff:
```python
import functools

import jax
import jax.numpy as jnp
from jax import lax
from jax.experimental import pallas as pl
from jax.experimental.pallas import tpu as pltpu
from jax.sharding import PartitionSpec as P

K = 512
BISECT = 6
MESH = pl.DeviceIdType.MESH
F32 = jnp.float32
BF16 = jnp.bfloat16
SEARCH = 512
INNER, OUTER = 16, 4
VMEM_LIMIT = 24 << 20


def mxu(a, b):
    return jnp.dot(a, b, preferred_element_type=F32)


def split(value):
    high = value.astype(BF16)
    return high, (value - high.astype(F32)).astype(BF16)


def apply_model(m_high, m_low, rest):
    high, low = split(rest)
    return mxu(m_high[...], high) + mxu(m_low[...], high) + mxu(m_high[...], low)


def column_fold(ref, place, change, fold):
    total = None
    for k in range(0, K, 8):
        value = change(ref[k:k + 8, place])
        total = value if total is None else fold(total, value)
    return total


def find_levels(shifted, levels):
    width = shifted.shape[1]
    for start in range(0, width, SEARCH):
        place = slice(start, start + SEARCH)
        same = lambda value: value

        def mass(level):
            wide = jnp.broadcast_to(level, (8, SEARCH))
            total = column_fold(shifted, place, lambda value: jnp.maximum(value, wide), jnp.add)
            return jnp.sum(total, axis=0, keepdims=True) - K * level

        high = jnp.max(column_fold(shifted, place, same, jnp.maximum), axis=0, keepdims=True)
        low = (jnp.sum(column_fold(shifted, place, same, jnp.add), axis=0, keepdims=True) - K) / K
        mass_low = mass(low)
        mass_high = jnp.zeros_like(high)
        for _ in range(BISECT):
            middle = 0.5 * (low + high)
            total = mass(middle)
            above = total > K
            low = jnp.where(above, middle, low)
            high = jnp.where(above, high, middle)
            mass_low = jnp.where(above, total, mass_low)
            mass_high = jnp.where(above, mass_high, total)
        levels[:, place] = low + (mass_low - K) * (high - low) / (mass_low - mass_high)


def lane_row(values):
    lane = lax.broadcasted_iota(jnp.int32, (1, 128), 1)
    row = jnp.zeros((1, 128), F32)
    for place, value in values:
        row = row + jnp.where(lane == place, jnp.sum(value, axis=1, keepdims=True), 0.0)
    return row


def square_sum(a, b):
    difference = a - b
    return jnp.sum(difference * difference, axis=0, keepdims=True)


def first_kernel(bands, padded, scale, spectra, endmembers, gram_hbm, z_hbm, u_hbm,
                 y_out, e_out, m_high, m_low, shifted, levels, sums,
                 gram, z_ref, u_ref, e_send, e_recv, y_send, y_recv, local_sem):
    me = lax.axis_index("band")
    rows = spectra.shape[0]
    columns = y_out.shape[1]
    mine = pl.ds(pl.multiple_of(me * padded, padded), rows)

    def spectra_of(band):
        return spectra.at[:, pl.ds(pl.multiple_of(band * columns, columns), columns)]

    peers = [lax.rem(me + step, bands) for step in range(1, bands)]
    barrier = pltpu.get_barrier_semaphore()
    for peer in peers:
        pl.semaphore_signal(barrier, inc=1, device_id={"band": peer}, device_id_type=MESH)
    own = [pltpu.make_async_copy(endmembers, e_out.at[mine, :], local_sem.at[0]),
           pltpu.make_async_copy(gram_hbm, gram, local_sem.at[1]),
           pltpu.make_async_copy(z_hbm, z_ref, local_sem.at[2]),
           pltpu.make_async_copy(u_hbm, u_ref, local_sem.at[3]),
           pltpu.make_async_copy(spectra_of(me), y_out.at[mine, :], local_sem.at[4])]
    for copy in own:
        copy.start()
    if padded > rows:
        for band in range(bands):
            start = band * padded + rows
            y_out[start:start + padded - rows, :] = jnp.zeros((padded - rows, columns), BF16)
            e_out[start:start + padded - rows, :] = jnp.zeros((padded - rows, K), BF16)
    pl.semaphore_wait(barrier, bands - 1)

    copies_e = [pltpu.make_async_remote_copy(
        src_ref=endmembers, dst_ref=e_out.at[mine, :], send_sem=e_send.at[step], recv_sem=e_recv.at[step],
        device_id={"band": peer}, device_id_type=MESH) for step, peer in enumerate(peers)]
    copies_y = [pltpu.make_async_remote_copy(
        src_ref=spectra_of(peer), dst_ref=y_out.at[mine, :], send_sem=y_send.at[step], recv_sem=y_recv.at[step],
        device_id={"band": peer}, device_id_type=MESH) for step, peer in enumerate(peers)]
    for copy in copies_e + copies_y:
        copy.start()

    for copy in own:
        copy.wait()
    for copy in copies_e:
        copy.wait_recv()
    signatures = e_out[...]
    total = jnp.zeros((K, bands * padded), F32)
    rest = gram[...]
    for _ in range(3):
        high = rest.astype(BF16)
        total += lax.dot_general(high, signatures, (((1,), (1,)), ((), ())), preferred_element_type=F32)
        rest = rest - high.astype(F32)
    m_high[...], m_low[...] = split(total * scale)
    high, low = split(z_ref[...] - u_ref[...])
    modelled = (mxu(signatures, high) + mxu(signatures, low)) * (1.0 / K)

    for copy in copies_y:
        copy.wait_recv()
    shifted[...] = z_ref[...] + apply_model(m_high, m_low, y_out[...].astype(F32) - modelled)
    find_levels(shifted, levels)
    value, level = shifted[...], levels[...]
    primal = square_sum(jnp.minimum(value, level), u_ref[...])
    change = square_sum(jnp.maximum(value - level, 0.0), z_ref[...])
    sums[...] = lane_row([(0, primal), (2, change)])
    for copy in copies_e + copies_y:
        copy.wait_send()


def second_kernel(bands, y_ref, e_ref, m_high, m_low, before, levels_before, sums,
                  shifted, levels, totals,
                  local, first, middle, second, send1, recv1, send2, recv2):
    pix, band = lax.axis_index("pix"), lax.axis_index("band")
    low_index, x = lax.rem(pix, INNER), pix // INNER
    place = x * bands + band

    def outer_target(step):
        other = lax.rem(place + step, OUTER * bands)
        return {"pix": (other // bands) * INNER + low_index, "band": lax.rem(other, bands)}

    targets1 = [{"pix": x * INNER + lax.rem(low_index + step, INNER), "band": band} for step in range(1, INNER)]
    targets2 = [outer_target(step) for step in range(1, OUTER * bands)]
    barrier = pltpu.get_barrier_semaphore()
    for target in targets1 + targets2:
        pl.semaphore_signal(barrier, inc=1, device_id=target, device_id_type=MESH)

    level_before = levels_before[...]
    high, low = split(jnp.abs(before[...] - level_before) - level_before)
    modelled = (mxu(e_ref[...], high) + mxu(e_ref[...], low)) * (1.0 / K)
    rest = y_ref[...].astype(F32) - modelled
    shifted[...] = jnp.maximum(before[...] - level_before, 0.0) + apply_model(m_high, m_low, rest)
    find_levels(shifted, levels)
    value, level, old = shifted[...], levels[...], before[...]
    primal = square_sum(jnp.minimum(value, level), jnp.minimum(old, level_before))
    change = square_sum(jnp.maximum(value - level, 0.0), jnp.maximum(old - level_before, 0.0))
    row = sums[...] + lane_row([(1, primal), (3, change)])
    local[...] = row
    first[0] = row

    pl.semaphore_wait(barrier, len(targets1) + len(targets2))
    copies1 = [pltpu.make_async_remote_copy(
        src_ref=local, dst_ref=first.at[step + 1], send_sem=send1.at[step], recv_sem=recv1.at[step],
        device_id=target, device_id_type=MESH) for step, target in enumerate(targets1)]
    for copy in copies1:
        copy.start()
    for copy in copies1:
        copy.wait_recv()
    row = jnp.sum(first[...], axis=0)
    middle[...] = row
    second[0] = row
    copies2 = [pltpu.make_async_remote_copy(
        src_ref=middle, dst_ref=second.at[step + 1], send_sem=send2.at[step], recv_sem=recv2.at[step],
        device_id=target, device_id_type=MESH) for step, target in enumerate(targets2)]
    for copy in copies2:
        copy.start()
    for copy in copies2:
        copy.wait_recv()
    totals[...] = jnp.sum(second[...], axis=0)
    for copy in copies1 + copies2:
        copy.wait_send()


def last_kernel(pixels, shifted, levels, totals, z_out, u_out, rms):
    level = levels[...]
    z_out[...] = jnp.maximum(shifted[...] - level, 0.0)
    u_out[...] = jnp.minimum(shifted[...], level)
    row = jnp.sqrt(totals[...] / pixels)
    rms[0:1, :] = row[:, 0:2]
    rms[1:2, :] = row[:, 2:4]


def body(bands, pixels, total_bands, spectra, endmembers, gram_inverse, abundances, duals):
    rows = spectra.shape[0]
    padded = -(-rows // 64) * 64
    depth = bands * padded
    columns = abundances.shape[1]
    penalty = total_bands / (2.0 * K * K)
    vmem = pl.BlockSpec(memory_space=pltpu.VMEM)
    hbm = pl.BlockSpec(memory_space=pltpu.HBM)
    shape = jax.ShapeDtypeStruct
    dma = pltpu.SemaphoreType.DMA
    y, e, m_high, m_low, shifted, levels, sums = pl.pallas_call(
        functools.partial(first_kernel, bands, padded, 1.0 / (K * penalty)),
        out_shape=(shape((depth, columns), BF16), shape((depth, K), BF16), shape((K, depth), BF16),
                   shape((K, depth), BF16), shape((K, columns), F32), shape((1, columns), F32), shape((1, 128), F32)),
        in_specs=[hbm] * 5,
        out_specs=(vmem,) * 7,
        scratch_shapes=[pltpu.VMEM((K, K), F32), pltpu.VMEM((K, columns), F32), pltpu.VMEM((K, columns), F32)]
        + [dma((bands - 1,))] * 4 + [dma((5,))],
        compiler_params=pltpu.CompilerParams(collective_id=0, has_side_effects=True, vmem_limit_bytes=VMEM_LIMIT),
        name="first",
    )(*[pltpu.with_memory_space_constraint(array, pltpu.HBM)
        for array in (spectra, endmembers, gram_inverse, abundances, duals)])
    n1, n2 = INNER, OUTER * bands
    shifted, levels, totals = pl.pallas_call(
        functools.partial(second_kernel, bands),
        out_shape=(shape((K, columns), F32), shape((1, columns), F32), shape((1, 128), F32)),
        in_specs=[vmem] * 7,
        out_specs=(vmem,) * 3,
        scratch_shapes=[pltpu.VMEM((1, 128), F32), pltpu.VMEM((n1, 1, 128), F32), pltpu.VMEM((1, 128), F32),
                        pltpu.VMEM((n2, 1, 128), F32), dma((n1,)), dma((n1,)), dma((n2,)), dma((n2,))],
        compiler_params=pltpu.CompilerParams(collective_id=1, has_side_effects=True, vmem_limit_bytes=VMEM_LIMIT),
        name="second",
    )(y, e, m_high, m_low, shifted, levels, sums)
    block = pl.BlockSpec((K // 4, columns), lambda i: (i, 0))
    whole = lambda i: (0, 0)
    return pl.pallas_call(
        functools.partial(last_kernel, pixels),
        grid=(4,),
        out_shape=(shape((K, columns), F32), shape((K, columns), F32), shape((2, 2), F32)),
        in_specs=[block, pl.BlockSpec((1, columns), whole), pl.BlockSpec((1, 128), whole)],
        out_specs=(block, block, pl.BlockSpec((2, 2), whole)),
        compiler_params=pltpu.CompilerParams(vmem_limit_bytes=VMEM_LIMIT),
        name="last",
    )(shifted, levels, totals)


def solution(mesh):
    bands = mesh.shape["band"]

    def run(spectra, endmembers, gram_inverse, abundances, duals):
        step = functools.partial(body, bands, abundances.shape[1], spectra.shape[0])
        return jax.shard_map(
            step,
            mesh=mesh,
            in_specs=(P("band", "pix"), P("band", None), P(), P(None, ("pix", "band")), P(None, ("pix", "band"))),
            out_specs=(P(None, ("pix", "band")), P(None, ("pix", "band")), P()),
            check_vma=False,
        )(spectra, endmembers, gram_inverse, abundances, duals)

    return run
```

time: 110 us -> 41.4 us (0.38)
  blocking collectives: 56.2 us -> 0 us
  Pallas kernels: 0 us -> 40.7 us
  other arithmetic: 27.9 us -> 0 us
  matrix products: 16.1 us -> 0 us
  starting transfers between devices: 5 us -> 0 us
  local copies, waits for them, and re-layouts: 2.93 us -> 0 us
    psum x4 -> x0, blocking collectives: 43.7 us -> none  [one_axis_at_a_time(): shard = lax.psum(shard, axis)]
    pallas_call x0 -> x3, Pallas kernels: none -> 40.7 us  [the longest x1 22 us: body(): pl.pallas_call(functools.partial(second_kernel, bands), out_shape=(shape(...]
    reduce_sum x15 -> x0, other arithmetic: 20.3 us -> none  [the longest x14 13.3 us: mass_at(): return jnp.sum(jnp.maximum(shifted - level[None, :], 0.0), axis=0)]
    dot_general x3 -> x0, matrix products: 16.1 us -> none  [the longest x2 15.7 us: body(): jnp.dot(gram_inverse, fit_term / penalty + current - scaled_dual, precisi...]
    all_gather x1 -> x0, blocking collectives: 12.5 us -> none  [body(): all_rows = lax.all_gather(endmembers, 'band', axis=0, tiled=True)]
    all_to_all x1 -> x0, starting transfers between devices: 5 us -> none  [body(): lax.all_to_all(spectra, 'band', split_axis=1, concat_axis=0, tiled=True)]
    sub x1 -> x0, other arithmetic: 4.1 us -> none  [body(): scaled_dual = scaled_dual + primal - updated]
    another operation x2 -> x0, other arithmetic: 2.64 us -> none  [body(): totals = jnp.stack([jnp.stack(primal_list), jnp.stack(change_list)])]
  transfers between devices with their start and end apart: 1 -> 0, of which waited for: 0 -> 0; matrix products, arithmetic and copies ran while one was open for 0% -> 0% of each run, Pallas kernels for 0% -> 0%
where the time goes in v2:
time: 41.4 us; the launch traced here: 41.3 us
  Pallas kernels  40.7 us (98%)
  between operations  0.65 us (2%)
    pallas_call x1, Pallas kernels, body(): pl.pallas_call(functools.partial(second_kernel, bands), out_shape=(shape(...  22 us
    pallas_call x1, Pallas kernels, body(): pl.pallas_call(functools.partial(first_kernel, bands, padded, 1.0 / (K *...  16.1 us
    pallas_call x1, Pallas kernels, body(): pl.pallas_call(functools.partial(last_kernel, pixels), grid=(4,), out_sha...  2.49 us

profile of v2, /device:TPU:1, one launch (start us, length us, event | category | flops | bytes accessed | tf_op | source)
XLA Modules:
  0.0 41.3 jit_solution(1248932025228528775)
XLA Ops:
  0.6 16.1 %first.1 = (bf16[256,1024]{1,0:T(8,128)(2,1)S(1)}, bf16[256,512]{1,0:T(8,128)(2,1)S(1)}, bf16[512,256]{1,0:T(8,128)(2,1)S(1)}, bf16[512,256]{1,0:T(8,128)(2,1)S(...) custom-call(bf16[56,4096]{1,0:T(8,128)(2,1)} %spectra.1, bf16[56,512]{1,0:T(8,128)(2,1)} %endmembers.1, ...), custom_call_target="tpu_custom_call" | custom-call | tf_op jit(solution)/shard_map/first/pallas_call | solution.py:218
  16.8 22.0 %second.1 = (f32[512,1024]{1,0:T(8,128)S(1)}, f32[1,1024]{1,0:T(1,128)S(1)}, f32[1,128]{1,0:T(1,128)S(1)}) custom-call(bf16[256,1024]{1,0:T(8,128)(2,1)S(1)} %get-tuple-element.13.y_ref, bf16[256,512]{1,0:T(8,128)(2,1)S(1)} %get-tuple-element.14.e_ref, bf16[512,256]{1,0:T(8,128)(2,1)S(1)} %get-tuple-element.15.m_high, ...), custom_call_target="tpu_custom_call" | custom-call | tf_op jit(solution)/shard_map/second/pallas_call | solution.py:231
  38.8 2.5 %last.1 = (f32[512,1024]{1,0:T(8,128)}, f32[512,1024]{1,0:T(8,128)}, f32[2,2]{1,0:T(2,128)}) custom-call(f32[512,1024]{1,0:T(8,128)S(1)} %get-tuple-element.20.shifted, f32[1,1024]{1,0:T(1,128)S(1)} %get-tuple-element.21.levels, f32[1,128]{1,0:T(1,128)S(1)} %get-tuple-element.22.totals), custom_call_target="tpu_custom_call" | custom-call | tf_op jit(solution)/shard_map/last/pallas_call | solution.py:243

commit v3 on v2

v3 whole, which is shorter than its diff:
```python
import functools

import jax
import jax.numpy as jnp
from jax import lax
from jax.experimental import pallas as pl
from jax.experimental.pallas import tpu as pltpu
from jax.sharding import PartitionSpec as P

K = 512
BISECT = 6
MESH = pl.DeviceIdType.MESH
F32 = jnp.float32
BF16 = jnp.bfloat16
SEARCH = 512
OUTER, LONG = 4, 8
PARTS = 2
VMEM_LIMIT = 24 << 20


def mxu(a, b):
    return jnp.dot(a, b, preferred_element_type=F32)


def split(value):
    high = value.astype(BF16)
    return high, (value - high.astype(F32)).astype(BF16)


def apply_model(m_high, m_low, rest):
    high, low = split(rest)
    return mxu(m_high[...], high) + mxu(m_low[...], high) + mxu(m_high[...], low)


def column_fold(ref, place, change, fold):
    total = None
    for k in range(0, K, 8):
        value = change(ref[k:k + 8, place])
        total = value if total is None else fold(total, value)
    return total


def find_levels(shifted, levels, begin, width):
    for start in range(begin, begin + width, SEARCH):
        place = slice(start, start + SEARCH)
        same = lambda value: value

        def mass(level):
            wide = jnp.broadcast_to(level, (8, SEARCH))
            total = column_fold(shifted, place, lambda value: jnp.maximum(value, wide), jnp.add)
            return jnp.sum(total, axis=0, keepdims=True) - K * level

        high = jnp.max(column_fold(shifted, place, same, jnp.maximum), axis=0, keepdims=True)
        low = (jnp.sum(column_fold(shifted, place, same, jnp.add), axis=0, keepdims=True) - K) / K
        mass_low = mass(low)
        mass_high = jnp.zeros_like(high)
        for _ in range(BISECT):
            middle = 0.5 * (low + high)
            total = mass(middle)
            above = total > K
            low = jnp.where(above, middle, low)
            high = jnp.where(above, high, middle)
            mass_low = jnp.where(above, total, mass_low)
            mass_high = jnp.where(above, mass_high, total)
        levels[:, place] = low + (mass_low - K) * (high - low) / (mass_low - mass_high)


def lane_row(values):
    lane = lax.broadcasted_iota(jnp.int32, (1, 128), 1)
    row = jnp.zeros((1, 128), F32)
    for place, value in values:
        row = row + jnp.where(lane == place, jnp.sum(value), 0.0)
    return row


def first_kernel(bands, padded, scale, spectra, endmembers, gram_hbm, z_hbm, u_hbm,
                 y_out, e_out, m_high, m_low, shifted, levels, sums,
                 gram, z_ref, u_ref, w_high, w_low, modelled, e_send, e_recv, f_send, f_recv, y_send, y_recv, local_sem):
    me, pix = lax.axis_index("band"), lax.axis_index("pix")
    core = lax.rem(pix, 2)
    sibling = {"pix": pix + 1 - 2 * core, "band": me}
    rows = spectra.shape[0]
    columns = y_out.shape[1]
    part = columns // PARTS
    half = pl.ds(pl.multiple_of(core * (K // 2), K // 2), K // 2)

    def rows_of(band):
        return pl.ds(pl.multiple_of(band * padded, padded), rows)

    def spectra_of(band, start, width):
        return spectra.at[:, pl.ds(pl.multiple_of(band * columns + start, 128), width)]

    peers = [lax.rem(me + step, bands) for step in range(1, bands)]
    sources = [lax.rem(me + bands - step, bands) for step in range(1, bands)]
    barrier = pltpu.get_barrier_semaphore()
    for target in [{"pix": pix, "band": peer} for peer in peers] + [sibling]:
        pl.semaphore_signal(barrier, inc=1, device_id=target, device_id_type=MESH)
    own = [pltpu.make_async_copy(z_hbm, z_ref, local_sem.at[0]),
           pltpu.make_async_copy(u_hbm, u_ref, local_sem.at[1]),
           pltpu.make_async_copy(gram_hbm, gram, local_sem.at[2]),
           pltpu.make_async_copy(endmembers, e_out.at[rows_of(me), :], local_sem.at[3]),
           pltpu.make_async_copy(spectra_of(me, 0, columns), y_out.at[rows_of(me), :], local_sem.at[4])]
    for copy in own:
        copy.start()
    if padded > rows:
        for band in range(bands):
            start = band * padded + rows
            y_out[start:start + padded - rows, :] = jnp.zeros((padded - rows, columns), BF16)
            e_out[start:start + padded - rows, :] = jnp.zeros((padded - rows, K), BF16)
    pl.semaphore_wait(barrier, bands)

    copies_e = [pltpu.make_async_remote_copy(
        src_ref=endmembers.at[:, half], dst_ref=e_out.at[rows_of(me), half],
        send_sem=e_send.at[step], recv_sem=e_recv.at[step],
        device_id={"pix": pix, "band": peer}, device_id_type=MESH) for step, peer in enumerate(peers)]
    copies_y = [[pltpu.make_async_remote_copy(
        src_ref=spectra_of(peer, start, part), dst_ref=y_out.at[rows_of(me), start:start + part],
        send_sem=y_send.at[start // part, step], recv_sem=y_recv.at[start // part, step],
        device_id={"pix": pix, "band": peer}, device_id_type=MESH) for step, peer in enumerate(peers)]
        for start in range(0, columns, part)]
    for copy in sum(copies_y, copies_e):
        copy.start()
    copies_f = [pltpu.make_async_remote_copy(
        src_ref=e_out.at[rows_of(source), half], dst_ref=e_out.at[rows_of(source), half],
        send_sem=f_send.at[step], recv_sem=f_recv.at[step],
        device_id=sibling, device_id_type=MESH) for step, source in enumerate(sources)]
    for arrival, copy in zip(copies_e, copies_f):
        arrival.wait_recv()
        copy.start()
    for copy in own:
        copy.wait()
    for k in range(0, K, 64):
        w_high[k:k + 64, :], w_low[k:k + 64, :] = split(z_ref[k:k + 64, :] - u_ref[k:k + 64, :])
    for copy in copies_f:
        copy.wait_recv()

    signatures = e_out[...]
    total = jnp.zeros((K, bands * padded), F32)
    rest = gram[...]
    for _ in range(3):
        high = rest.astype(BF16)
        total += lax.dot_general(high, signatures, (((1,), (1,)), ((), ())), preferred_element_type=F32)
        rest = rest - high.astype(F32)
    m_high[...], m_low[...] = split(total * scale)
    modelled[...] = (mxu(signatures, w_high[...]) + mxu(signatures, w_low[...])) * (1.0 / K)

    values = []
    for index, start in enumerate(range(0, columns, part)):
        for copy in copies_y[index]:
            copy.wait_recv()
        place = slice(start, start + part)
        rest = y_out[:, place].astype(F32) - modelled[:, place]
        shifted[:, place] = z_ref[:, place] + apply_model(m_high, m_low, rest)
        find_levels(shifted, levels, start, part)
        level = jnp.broadcast_to(levels[:, place], (8, part))
        primal, change = jnp.zeros((8, part), F32), jnp.zeros((8, part), F32)
        for k in range(0, K, 8):
            value = shifted[k:k + 8, place]
            primal += jnp.square(jnp.minimum(value, level) - u_ref[k:k + 8, place])
            change += jnp.square(jnp.maximum(value - level, 0.0) - z_ref[k:k + 8, place])
        values += [(0, primal), (2, change)]
    sums[...] = lane_row(values)
    for copy in sum(copies_y, copies_e + copies_f):
        copy.wait_send()


def second_kernel(y_ref, e_ref, m_high, m_low, before, levels_before, sums_before, z_out, u_out, sums,
                  w_high, w_low, shifted, levels):
    columns = before.shape[1]
    level_before = levels_before[...]
    for k in range(0, K, 64):
        w_high[k:k + 64, :], w_low[k:k + 64, :] = split(jnp.abs(before[k:k + 64, :] - level_before) - level_before)
    modelled = (mxu(e_ref[...], w_high[...]) + mxu(e_ref[...], w_low[...])) * (1.0 / K)
    rest = y_ref[...].astype(F32) - modelled
    shifted[...] = jnp.maximum(before[...] - level_before, 0.0) + apply_model(m_high, m_low, rest)
    find_levels(shifted, levels, 0, columns)
    values = []
    for start in range(0, columns, SEARCH):
        place = slice(start, start + SEARCH)
        level = jnp.broadcast_to(levels[:, place], (8, SEARCH))
        old = jnp.broadcast_to(levels_before[:, place], (8, SEARCH))
        primal, change = jnp.zeros((8, SEARCH), F32), jnp.zeros((8, SEARCH), F32)
        for k in range(0, K, 8):
            value, earlier = shifted[k:k + 8, place], before[k:k + 8, place]
            z, u = jnp.maximum(value - level, 0.0), jnp.minimum(value, level)
            z_out[k:k + 8, place] = z
            u_out[k:k + 8, place] = u
            primal += jnp.square(u - jnp.minimum(earlier, old))
            change += jnp.square(z - jnp.maximum(earlier - old, 0.0))
        values += [(1, primal), (3, change)]
    sums[...] = sums_before[...] + lane_row(values)


def ring_distance(step, size):
    return min(step, size - step)


def reduce_kernel(bands, mine, totals, first, middle, second, send1, recv1, send2, recv2):
    pix, band = lax.axis_index("pix"), lax.axis_index("band")
    core, z, x = lax.rem(pix, 2), lax.rem(pix // 2, LONG), pix // (2 * LONG)
    steps1 = sorted(((dz, dc) for dz in range(LONG) for dc in range(2) if dz or dc),
                    key=lambda s: -ring_distance(s[0], LONG) * 2 - s[1])
    steps2 = sorted(((dx, dy) for dx in range(OUTER) for dy in range(bands) if dx or dy),
                    key=lambda s: -ring_distance(s[0], OUTER) - ring_distance(s[1], bands))
    targets1 = [{"pix": (x * LONG + lax.rem(z + dz, LONG)) * 2 + lax.rem(core + dc, 2), "band": band}
                for dz, dc in steps1]
    targets2 = [{"pix": (lax.rem(x + dx, OUTER) * LONG + z) * 2 + core, "band": lax.rem(band + dy, bands)}
                for dx, dy in steps2]
    barrier = pltpu.get_barrier_semaphore()
    for target in targets2 + targets1:
        pl.semaphore_signal(barrier, inc=1, device_id=target, device_id_type=MESH)
    first[0] = mine[...]
    pl.semaphore_wait(barrier, len(targets1) + len(targets2))

    def exchange(source, slots, send, recv, targets):
        for step, target in enumerate(targets):
            pltpu.make_async_remote_copy(src_ref=source, dst_ref=slots.at[step + 1], send_sem=send, recv_sem=recv,
                                         device_id=target, device_id_type=MESH).start()
        filled = slots.at[1:len(targets) + 1]
        pltpu.make_async_copy(filled, filled, recv).wait()

    exchange(mine, first, send1, recv1, targets1)
    row = jnp.sum(first[...], axis=0)
    middle[...] = row
    second[0] = row
    exchange(middle, second, send2, recv2, targets2)
    totals[...] = jnp.sum(second[...], axis=0)
    for slots, send, targets in ((first, send1, targets1), (second, send2, targets2)):
        filled = slots.at[1:len(targets) + 1]
        pltpu.make_async_copy(filled, filled, send).wait()


def last_kernel(pixels, totals, rms):
    row = jnp.sqrt(totals[...] / pixels)
    rms[0:1, :] = row[:, 0:2]
    rms[1:2, :] = row[:, 2:4]


def body(bands, pixels, total_bands, spectra, endmembers, gram_inverse, abundances, duals):
    rows = spectra.shape[0]
    padded = -(-rows // 64) * 64
    depth = bands * padded
    columns = abundances.shape[1]
    penalty = total_bands / (2.0 * K * K)
    vmem = pl.BlockSpec(memory_space=pltpu.VMEM)
    hbm = pl.BlockSpec(memory_space=pltpu.HBM)
    shape = jax.ShapeDtypeStruct
    dma = pltpu.SemaphoreType.DMA
    square, wide = shape((K, columns), F32), shape((1, columns), F32)
    line = shape((1, 128), F32)
    big = pltpu.VMEM((K, columns), F32)
    packed = pltpu.VMEM((K, columns), BF16)
    y, e, m_high, m_low, shifted, levels, sums = pl.pallas_call(
        functools.partial(first_kernel, bands, padded, 1.0 / (K * penalty)),
        out_shape=(shape((depth, columns), BF16), shape((depth, K), BF16), shape((K, depth), BF16),
                   shape((K, depth), BF16), square, wide, line),
        in_specs=[hbm] * 5,
        out_specs=(vmem,) * 7,
        scratch_shapes=[pltpu.VMEM((K, K), F32), big, big, packed, packed, pltpu.VMEM((depth, columns), F32)]
        + [dma((bands - 1,))] * 4 + [dma((PARTS, bands - 1))] * 2 + [dma((5,))],
        compiler_params=pltpu.CompilerParams(collective_id=0, has_side_effects=True, vmem_limit_bytes=VMEM_LIMIT),
        name="first",
    )(*[pltpu.with_memory_space_constraint(array, pltpu.HBM)
        for array in (spectra, endmembers, gram_inverse, abundances, duals)])
    z, u, sums = pl.pallas_call(
        second_kernel,
        out_shape=(square, square, line),
        in_specs=[vmem] * 7,
        out_specs=(vmem,) * 3,
        scratch_shapes=[packed, packed, big, pltpu.VMEM((1, columns), F32)],
        compiler_params=pltpu.CompilerParams(vmem_limit_bytes=VMEM_LIMIT),
        name="second",
    )(y, e, m_high, m_low, shifted, levels, sums)
    n1, n2 = 2 * LONG, OUTER * bands
    totals = pl.pallas_call(
        functools.partial(reduce_kernel, bands),
        out_shape=line,
        in_specs=[vmem],
        out_specs=vmem,
        scratch_shapes=[pltpu.VMEM((n1, 1, 128), F32), pltpu.VMEM((1, 128), F32), pltpu.VMEM((n2, 1, 128), F32)]
        + [dma] * 4,
        compiler_params=pltpu.CompilerParams(collective_id=1, has_side_effects=True, vmem_limit_bytes=VMEM_LIMIT),
        name="reduce",
    )(sums)
    rms = pl.pallas_call(
        functools.partial(last_kernel, pixels),
        out_shape=shape((2, 2), F32),
        in_specs=[vmem],
        out_specs=vmem,
        compiler_params=pltpu.CompilerParams(vmem_limit_bytes=VMEM_LIMIT),
        name="last",
    )(totals)
    return z, u, rms


def solution(mesh):
    bands = mesh.shape["band"]

    def run(spectra, endmembers, gram_inverse, abundances, duals):
        step = functools.partial(body, bands, abundances.shape[1], spectra.shape[0])
        return jax.shard_map(
            step,
            mesh=mesh,
            in_specs=(P("band", "pix"), P("band", None), P(), P(None, ("pix", "band")), P(None, ("pix", "band"))),
            out_specs=(P(None, ("pix", "band")), P(None, ("pix", "band")), P()),
            check_vma=False,
        )(spectra, endmembers, gram_inverse, abundances, duals)

    return run
```

time: 41.4 us -> 39.4 us (0.952)
  Pallas kernels: 40.7 us -> 38.7 us
    pallas_call x2 -> x3, Pallas kernels: 24.5 us -> 22.2 us  [the longest x1 15.2 us: body(): pl.pallas_call(functools.partial(reduce_kernel, bands), out_shape=line, i...]
where the time goes in v3:
time: 39.4 us; the launch traced here: 39.3 us
  Pallas kernels  38.7 us (98%)
  between operations  0.65 us (2%)
    pallas_call x1, Pallas kernels, body(): pl.pallas_call(functools.partial(first_kernel, bands, padded, 1.0 / (K *...  16.5 us
    pallas_call x1, Pallas kernels, body(): pl.pallas_call(functools.partial(reduce_kernel, bands), out_shape=line, i...  15.2 us
    pallas_call x1, Pallas kernels, body(): pl.pallas_call(second_kernel, out_shape=(square, square, line), in_specs=...  6.38 us

profile of v3, /device:TPU:1, one launch (start us, length us, event | category | flops | bytes accessed | tf_op | source)
XLA Modules:
  0.0 39.3 jit_solution(4750671519874827897)
XLA Ops:
  0.6 16.5 %first.1 = (bf16[256,1024]{1,0:T(8,128)(2,1)S(1)}, bf16[256,512]{1,0:T(8,128)(2,1)S(1)}, bf16[512,256]{1,0:T(8,128)(2,1)S(1)}, bf16[512,256]{1,0:T(8,128)(2,1)S(...) custom-call(bf16[56,4096]{1,0:T(8,128)(2,1)} %spectra.1, bf16[56,512]{1,0:T(8,128)(2,1)} %endmembers.1, ...), custom_call_target="tpu_custom_call" | custom-call | tf_op jit(solution)/shard_map/first/pallas_call | solution.py:253
  17.1 6.4 %second.1 = (f32[512,1024]{1,0:T(8,128)}, f32[512,1024]{1,0:T(8,128)}, f32[1,128]{1,0:T(1,128)S(1)}) custom-call(bf16[256,1024]{1,0:T(8,128)(2,1)S(1)} %get-tuple-element.13.y_ref, bf16[256,512]{1,0:T(8,128)(2,1)S(1)} %get-tuple-element.14.e_ref, bf16[512,256]{1,0:T(8,128)(2,1)S(1)} %get-tuple-element.15.m_high, ...), custom_call_target="tpu_custom_call" | custom-call | tf_op jit(solution)/shard_map/second/pallas_call | solution.py:265
  23.5 15.2 %reduce.1.totals = f32[1,128]{1,0:T(1,128)S(1)} custom-call(f32[1,128]{1,0:T(1,128)S(1)} %get-tuple-element.22.mine), custom_call_target="tpu_custom_call" | custom-call | tf_op jit(solution)/shard_map/reduce/pallas_call | solution.py:275
  38.7 0.6 %last.1 = f32[2,2]{1,0:T(2,128)} custom-call(f32[1,128]{1,0:T(1,128)S(1)} %reduce.1.totals), custom_call_target="tpu_custom_call" | custom-call | tf_op jit(solution)/shard_map/last/pallas_call | solution.py:285

commit v4 on v3

--- a/solution.py
+++ b/solution.py
@@ -75,7 +75,7 @@
 
 def first_kernel(bands, padded, scale, spectra, endmembers, gram_hbm, z_hbm, u_hbm,
                  y_out, e_out, m_high, m_low, shifted, levels, sums,
-                 gram, z_ref, u_ref, w_high, w_low, modelled, e_send, e_recv, f_send, f_recv, y_send, y_recv, local_sem):
+                 gram, z_ref, u_ref, w_high, w_low, e_send, e_recv, f_send, f_recv, y_send, y_recv, local_sem):
     me, pix = lax.axis_index("band"), lax.axis_index("pix")
     core = lax.rem(pix, 2)
     sibling = {"pix": pix + 1 - 2 * core, "band": me}
@@ -124,13 +124,18 @@
         src_ref=e_out.at[rows_of(source), half], dst_ref=e_out.at[rows_of(source), half],
         send_sem=f_send.at[step], recv_sem=f_recv.at[step],
         device_id=sibling, device_id_type=MESH) for step, source in enumerate(sources)]
-    for arrival, copy in zip(copies_e, copies_f):
-        arrival.wait_recv()
-        copy.start()
     for copy in own:
         copy.wait()
     for k in range(0, K, 64):
         w_high[k:k + 64, :], w_low[k:k + 64, :] = split(z_ref[k:k + 64, :] - u_ref[k:k + 64, :])
+    g_high, g_low = split(gram[...])
+    for start in range(0, columns, part):
+        place = slice(start, start + part)
+        high = w_high[:, place]
+        shifted[:, place] = u_ref[:, place] + (mxu(g_high, high) + mxu(g_low, high) + mxu(g_high, w_low[:, place]))
+    for arrival, copy in zip(copies_e, copies_f):
+        arrival.wait_recv()
+        copy.start()
     for copy in copies_f:
         copy.wait_recv()
 
@@ -142,15 +147,14 @@
         total += lax.dot_general(high, signatures, (((1,), (1,)), ((), ())), preferred_element_type=F32)
         rest = rest - high.astype(F32)
     m_high[...], m_low[...] = split(total * scale)
-    modelled[...] = (mxu(signatures, w_high[...]) + mxu(signatures, w_low[...])) * (1.0 / K)
 
     values = []
     for index, start in enumerate(range(0, columns, part)):
         for copy in copies_y[index]:
             copy.wait_recv()
         place = slice(start, start + part)
-        rest = y_out[:, place].astype(F32) - modelled[:, place]
-        shifted[:, place] = z_ref[:, place] + apply_model(m_high, m_low, rest)
+        arrived = y_out[:, place]
+        shifted[:, place] += mxu(m_high[...], arrived) + mxu(m_low[...], arrived)
         find_levels(shifted, levels, start, part)
         level = jnp.broadcast_to(levels[:, place], (8, part))
         primal, change = jnp.zeros((8, part), F32), jnp.zeros((8, part), F32)
@@ -164,8 +168,8 @@
         copy.wait_send()
 
 
-def second_kernel(y_ref, e_ref, m_high, m_low, before, levels_before, sums_before, z_out, u_out, sums,
-                  w_high, w_low, shifted, levels):
+def second_kernel(y_ref, e_ref, m_high, m_low, before, levels_before, sums_before, z_hbm, u_hbm, sums,
+                  w_high, w_low, shifted, levels, z_out, u_out, out_sem):
     columns = before.shape[1]
     level_before = levels_before[...]
     for k in range(0, K, 64):
@@ -173,9 +177,9 @@
     modelled = (mxu(e_ref[...], w_high[...]) + mxu(e_ref[...], w_low[...])) * (1.0 / K)
     rest = y_ref[...].astype(F32) - modelled
     shifted[...] = jnp.maximum(before[...] - level_before, 0.0) + apply_model(m_high, m_low, rest)
-    find_levels(shifted, levels, 0, columns)
-    values = []
-    for start in range(0, columns, SEARCH):
+    values, copies = [], []
+    for index, start in enumerate(range(0, columns, SEARCH)):
+        find_levels(shifted, levels, start, SEARCH)
         place = slice(start, start + SEARCH)
         level = jnp.broadcast_to(levels[:, place], (8, SEARCH))
         old = jnp.broadcast_to(levels_before[:, place], (8, SEARCH))
@@ -188,7 +192,12 @@
             primal += jnp.square(u - jnp.minimum(earlier, old))
             change += jnp.square(z - jnp.maximum(earlier - old, 0.0))
         values += [(1, primal), (3, change)]
+        for which, (source, target) in enumerate(((z_out, z_hbm), (u_out, u_hbm))):
+            copies.append(pltpu.make_async_copy(source.at[:, place], target.at[:, place], out_sem.at[index, which]))
+            copies[-1].start()
     sums[...] = sums_before[...] + lane_row(values)
+    for copy in copies:
+        copy.wait()
 
 
 def ring_distance(step, size):
@@ -256,7 +265,7 @@
                    shape((K, depth), BF16), square, wide, line),
         in_specs=[hbm] * 5,
         out_specs=(vmem,) * 7,
-        scratch_shapes=[pltpu.VMEM((K, K), F32), big, big, packed, packed, pltpu.VMEM((depth, columns), F32)]
+        scratch_shapes=[pltpu.VMEM((K, K), F32), big, big, packed, packed]
         + [dma((bands - 1,))] * 4 + [dma((PARTS, bands - 1))] * 2 + [dma((5,))],
         compiler_params=pltpu.CompilerParams(collective_id=0, has_side_effects=True, vmem_limit_bytes=VMEM_LIMIT),
         name="first",
@@ -266,8 +275,8 @@
         second_kernel,
         out_shape=(square, square, line),
         in_specs=[vmem] * 7,
-        out_specs=(vmem,) * 3,
-        scratch_shapes=[packed, packed, big, pltpu.VMEM((1, columns), F32)],
+        out_specs=(hbm, hbm, vmem),
+        scratch_shapes=[packed, packed, big, pltpu.VMEM((1, columns), F32), big, big, dma((columns // SEARCH, 2))],
         compiler_params=pltpu.CompilerParams(vmem_limit_bytes=VMEM_LIMIT),
         name="second",
     )(y, e, m_high, m_low, shifted, levels, sums)

time: 39.4 us -> 38.6 us (0.980)
  Pallas kernels: 38.7 us -> 37.9 us
    pallas_call x1, Pallas kernels: 16.5 us -> 15.4 us  [body(): pl.pallas_call(functools.partial(first_kernel, bands, padded, 1.0 / (K *...]
    pallas_call x1, Pallas kernels: 15.2 us -> 15.7 us  [body(): pl.pallas_call(functools.partial(reduce_kernel, bands), out_shape=line, i...]
where the time goes in v4:
time: 38.6 us; the launch traced here: 38.5 us
  Pallas kernels  37.9 us (98%)
  between operations  0.66 us (2%)
    pallas_call x1, Pallas kernels, body(): pl.pallas_call(functools.partial(reduce_kernel, bands), out_shape=line, i...  15.7 us
    pallas_call x1, Pallas kernels, body(): pl.pallas_call(functools.partial(first_kernel, bands, padded, 1.0 / (K *...  15.4 us
    pallas_call x1, Pallas kernels, body(): pl.pallas_call(second_kernel, out_shape=(square, square, line), in_specs=...  6.13 us

profile of v4, /device:TPU:1, one launch (start us, length us, event | category | flops | bytes accessed | tf_op | source)
XLA Modules:
  0.0 38.5 jit_solution(15610640399303768986)
XLA Ops:
  0.6 15.4 %first.1 = (bf16[256,1024]{1,0:T(8,128)(2,1)S(1)}, bf16[256,512]{1,0:T(8,128)(2,1)S(1)}, bf16[512,256]{1,0:T(8,128)(2,1)S(1)}, bf16[512,256]{1,0:T(8,128)(2,1)S(...) custom-call(bf16[56,4096]{1,0:T(8,128)(2,1)} %spectra.1, bf16[56,512]{1,0:T(8,128)(2,1)} %endmembers.1, ...), custom_call_target="tpu_custom_call" | custom-call | tf_op jit(solution)/shard_map/first/pallas_call | solution.py:262
  16.0 6.1 %second.1 = (f32[512,1024]{1,0:T(8,128)}, f32[512,1024]{1,0:T(8,128)}, f32[1,128]{1,0:T(1,128)S(1)}) custom-call(bf16[256,1024]{1,0:T(8,128)(2,1)S(1)} %get-tuple-element.13.y_ref, bf16[256,512]{1,0:T(8,128)(2,1)S(1)} %get-tuple-element.14.e_ref, bf16[512,256]{1,0:T(8,128)(2,1)S(1)} %get-tuple-element.15.m_high, ...), custom_call_target="tpu_custom_call" | custom-call | tf_op jit(solution)/shard_map/second/pallas_call | solution.py:274
  22.2 15.7 %reduce.1.totals = f32[1,128]{1,0:T(1,128)S(1)} custom-call(f32[1,128]{1,0:T(1,128)S(1)} %get-tuple-element.22.mine), custom_call_target="tpu_custom_call" | custom-call | tf_op jit(solution)/shard_map/reduce/pallas_call | solution.py:284
  37.9 0.6 %last.1 = f32[2,2]{1,0:T(2,128)} custom-call(f32[1,128]{1,0:T(1,128)S(1)} %reduce.1.totals), custom_call_target="tpu_custom_call" | custom-call | tf_op jit(solution)/shard_map/last/pallas_call | solution.py:294

commit v5 on v4

--- a/solution.py
+++ b/solution.py
@@ -14,6 +14,7 @@
 BF16 = jnp.bfloat16
 SEARCH = 512
 OUTER, LONG = 4, 8
+OUT_PIECES = 4
 PARTS = 2
 VMEM_LIMIT = 24 << 20
 
@@ -168,43 +169,12 @@
         copy.wait_send()
 
 
-def second_kernel(y_ref, e_ref, m_high, m_low, before, levels_before, sums_before, z_hbm, u_hbm, sums,
-                  w_high, w_low, shifted, levels, z_out, u_out, out_sem):
-    columns = before.shape[1]
-    level_before = levels_before[...]
-    for k in range(0, K, 64):
-        w_high[k:k + 64, :], w_low[k:k + 64, :] = split(jnp.abs(before[k:k + 64, :] - level_before) - level_before)
-    modelled = (mxu(e_ref[...], w_high[...]) + mxu(e_ref[...], w_low[...])) * (1.0 / K)
-    rest = y_ref[...].astype(F32) - modelled
-    shifted[...] = jnp.maximum(before[...] - level_before, 0.0) + apply_model(m_high, m_low, rest)
-    values, copies = [], []
-    for index, start in enumerate(range(0, columns, SEARCH)):
-        find_levels(shifted, levels, start, SEARCH)
-        place = slice(start, start + SEARCH)
-        level = jnp.broadcast_to(levels[:, place], (8, SEARCH))
-        old = jnp.broadcast_to(levels_before[:, place], (8, SEARCH))
-        primal, change = jnp.zeros((8, SEARCH), F32), jnp.zeros((8, SEARCH), F32)
-        for k in range(0, K, 8):
-            value, earlier = shifted[k:k + 8, place], before[k:k + 8, place]
-            z, u = jnp.maximum(value - level, 0.0), jnp.minimum(value, level)
-            z_out[k:k + 8, place] = z
-            u_out[k:k + 8, place] = u
-            primal += jnp.square(u - jnp.minimum(earlier, old))
-            change += jnp.square(z - jnp.maximum(earlier - old, 0.0))
-        values += [(1, primal), (3, change)]
-        for which, (source, target) in enumerate(((z_out, z_hbm), (u_out, u_hbm))):
-            copies.append(pltpu.make_async_copy(source.at[:, place], target.at[:, place], out_sem.at[index, which]))
-            copies[-1].start()
-    sums[...] = sums_before[...] + lane_row(values)
-    for copy in copies:
-        copy.wait()
-
-
 def ring_distance(step, size):
     return min(step, size - step)
 
 
-def reduce_kernel(bands, mine, totals, first, middle, second, send1, recv1, send2, recv2):
+def second_kernel(bands, y_ref, e_ref, m_high, m_low, before, levels_before, sums_before, z_out, u_out, totals,
+                  w_high, w_low, shifted, levels, mine, first, middle, second, send1, recv1, send2, recv2):
     pix, band = lax.axis_index("pix"), lax.axis_index("band")
     core, z, x = lax.rem(pix, 2), lax.rem(pix // 2, LONG), pix // (2 * LONG)
     steps1 = sorted(((dz, dc) for dz in range(LONG) for dc in range(2) if dz or dc),
@@ -218,7 +188,32 @@
     barrier = pltpu.get_barrier_semaphore()
     for target in targets2 + targets1:
         pl.semaphore_signal(barrier, inc=1, device_id=target, device_id_type=MESH)
-    first[0] = mine[...]
+
+    columns = before.shape[1]
+    level_before = levels_before[...]
+    for k in range(0, K, 64):
+        w_high[k:k + 64, :], w_low[k:k + 64, :] = split(jnp.abs(before[k:k + 64, :] - level_before) - level_before)
+    modelled = (mxu(e_ref[...], w_high[...]) + mxu(e_ref[...], w_low[...])) * (1.0 / K)
+    rest = y_ref[...].astype(F32) - modelled
+    shifted[...] = jnp.maximum(before[...] - level_before, 0.0) + apply_model(m_high, m_low, rest)
+    find_levels(shifted, levels, 0, columns)
+    values = []
+    for start in range(0, columns, SEARCH):
+        place = slice(start, start + SEARCH)
+        level = jnp.broadcast_to(levels[:, place], (8, SEARCH))
+        old = jnp.broadcast_to(levels_before[:, place], (8, SEARCH))
+        primal, change = jnp.zeros((8, SEARCH), F32), jnp.zeros((8, SEARCH), F32)
+        for k in range(0, K, 8):
+            value, earlier = shifted[k:k + 8, place], before[k:k + 8, place]
+            z_new, u_new = jnp.maximum(value - level, 0.0), jnp.minimum(value, level)
+            z_out[k:k + 8, place] = z_new
+            u_out[k:k + 8, place] = u_new
+            primal += jnp.square(u_new - jnp.minimum(earlier, old))
+            change += jnp.square(z_new - jnp.maximum(earlier - old, 0.0))
+        values += [(1, primal), (3, change)]
+    row = sums_before[...] + lane_row(values)
+    mine[...] = row
+    first[0] = row
     pl.semaphore_wait(barrier, len(targets1) + len(targets2))
 
     def exchange(source, slots, send, recv, targets):
@@ -239,10 +234,18 @@
         pltpu.make_async_copy(filled, filled, send).wait()
 
 
-def last_kernel(pixels, totals, rms):
+def last_kernel(pixels, z, u, totals, z_out, u_out, rms, sem):
+    copies = []
+    for piece in range(OUT_PIECES):
+        rows = slice(piece * (K // OUT_PIECES), (piece + 1) * (K // OUT_PIECES))
+        for which, (source, target) in enumerate(((z, z_out), (u, u_out))):
+            copies.append(pltpu.make_async_copy(source.at[rows, :], target.at[rows, :], sem.at[piece, which]))
+            copies[-1].start()
     row = jnp.sqrt(totals[...] / pixels)
     rms[0:1, :] = row[:, 0:2]
     rms[1:2, :] = row[:, 2:4]
+    for copy in copies:
+        copy.wait()
 
 
 def body(bands, pixels, total_bands, spectra, endmembers, gram_inverse, abundances, duals):
@@ -271,35 +274,28 @@
         name="first",
     )(*[pltpu.with_memory_space_constraint(array, pltpu.HBM)
         for array in (spectra, endmembers, gram_inverse, abundances, duals)])
-    z, u, sums = pl.pallas_call(
-        second_kernel,
-        out_shape=(square, square, line),
+    n1, n2 = 2 * LONG, OUTER * bands
+    resident = pltpu.VMEM((K, columns), F32)
+    z, u, totals = pl.pallas_call(
+        functools.partial(second_kernel, bands),
+        out_shape=(resident, resident, line),
         in_specs=[vmem] * 7,
-        out_specs=(hbm, hbm, vmem),
-        scratch_shapes=[packed, packed, big, pltpu.VMEM((1, columns), F32), big, big, dma((columns // SEARCH, 2))],
-        compiler_params=pltpu.CompilerParams(vmem_limit_bytes=VMEM_LIMIT),
+        out_specs=(vmem,) * 3,
+        scratch_shapes=[packed, packed, big, pltpu.VMEM((1, columns), F32), pltpu.VMEM((1, 128), F32),
+                        pltpu.VMEM((n1, 1, 128), F32), pltpu.VMEM((1, 128), F32), pltpu.VMEM((n2, 1, 128), F32)]
+        + [dma] * 4,
+        compiler_params=pltpu.CompilerParams(collective_id=1, has_side_effects=True, vmem_limit_bytes=VMEM_LIMIT),
         name="second",
     )(y, e, m_high, m_low, shifted, levels, sums)
-    n1, n2 = 2 * LONG, OUTER * bands
-    totals = pl.pallas_call(
-        functools.partial(reduce_kernel, bands),
-        out_shape=line,
-        in_specs=[vmem],
-        out_specs=vmem,
-        scratch_shapes=[pltpu.VMEM((n1, 1, 128), F32), pltpu.VMEM((1, 128), F32), pltpu.VMEM((n2, 1, 128), F32)]
-        + [dma] * 4,
-        compiler_params=pltpu.CompilerParams(collective_id=1, has_side_effects=True, vmem_limit_bytes=VMEM_LIMIT),
-        name="reduce",
-    )(sums)
-    rms = pl.pallas_call(
+    return pl.pallas_call(
         functools.partial(last_kernel, pixels),
-        out_shape=shape((2, 2), F32),
-        in_specs=[vmem],
-        out_specs=vmem,
+        out_shape=(square, square, shape((2, 2), F32)),
+        in_specs=[vmem] * 3,
+        out_specs=(hbm, hbm, vmem),
+        scratch_shapes=[dma((OUT_PIECES, 2))],
         compiler_params=pltpu.CompilerParams(vmem_limit_bytes=VMEM_LIMIT),
         name="last",
-    )(totals)
-    return z, u, rms
+    )(z, u, totals)
 
 
 def solution(mesh):

time: 38.6 us -> 37.3 us (0.966)
  Pallas kernels: 37.9 us -> 36.6 us
    pallas_call x3 -> x2, Pallas kernels: 22.5 us -> 21.2 us  [the longest x1 18.5 us: body(): pl.pallas_call(functools.partial(second_kernel, bands), out_shape=(reside...]
where the time goes in v5:
time: 37.3 us; the launch traced here: 37.2 us
  Pallas kernels  36.6 us (98%)
  between operations  0.65 us (2%)
    pallas_call x1, Pallas kernels, body(): pl.pallas_call(functools.partial(second_kernel, bands), out_shape=(reside...  18.5 us
    pallas_call x1, Pallas kernels, body(): pl.pallas_call(functools.partial(first_kernel, bands, padded, 1.0 / (K *...  15.4 us
    pallas_call x1, Pallas kernels, body(): pl.pallas_call(functools.partial(last_kernel, pixels), out_shape=(square,...  2.63 us

profile of v5, /device:TPU:1, one launch (start us, length us, event | category | flops | bytes accessed | tf_op | source)
XLA Modules:
  0.0 37.2 jit_solution(7394605346373151071)
XLA Ops:
  0.6 15.4 %first.1 = (bf16[256,1024]{1,0:T(8,128)(2,1)S(1)}, bf16[256,512]{1,0:T(8,128)(2,1)S(1)}, bf16[512,256]{1,0:T(8,128)(2,1)S(1)}, bf16[512,256]{1,0:T(8,128)(2,1)S(...) custom-call(bf16[56,4096]{1,0:T(8,128)(2,1)} %spectra.1, bf16[56,512]{1,0:T(8,128)(2,1)} %endmembers.1, ...), custom_call_target="tpu_custom_call" | custom-call | tf_op jit(solution)/shard_map/first/pallas_call | solution.py:265
  16.0 18.5 %second.1 = (f32[512,1024]{1,0:T(8,128)S(1)}, f32[512,1024]{1,0:T(8,128)S(1)}, f32[1,128]{1,0:T(1,128)S(1)}) custom-call(bf16[256,1024]{1,0:T(8,128)(2,1)S(1)} %get-tuple-element.13.y_ref, bf16[256,512]{1,0:T(8,128)(2,1)S(1)} %get-tuple-element.14.e_ref, bf16[512,256]{1,0:T(8,128)(2,1)S(1)} %get-tuple-element.15.m_high, ...), custom_call_target="tpu_custom_call" | custom-call | tf_op jit(solution)/shard_map/second/pallas_call | solution.py:279
  34.6 2.6 %last.1 = (f32[512,1024]{1,0:T(8,128)}, f32[512,1024]{1,0:T(8,128)}, f32[2,2]{1,0:T(2,128)}) custom-call(f32[512,1024]{1,0:T(8,128)S(1)} %get-tuple-element.20.z, f32[512,1024]{1,0:T(8,128)S(1)} %get-tuple-element.21.u, f32[1,128]{1,0:T(1,128)S(1)} %get-tuple-element.22.totals), custom_call_target="tpu_custom_call" | custom-call | tf_op jit(solution)/shard_map/last/pallas_call | solution.py:290

commit v6 on v5

--- a/solution.py
+++ b/solution.py
@@ -15,7 +15,7 @@
 SEARCH = 512
 OUTER, LONG = 4, 8
 OUT_PIECES = 4
-PARTS = 2
+EDGES = (0, 5, 8)
 VMEM_LIMIT = 24 << 20
 
 
@@ -41,48 +41,63 @@
     return total
 
 
-def find_levels(shifted, levels, begin, width):
-    for start in range(begin, begin + width, SEARCH):
-        place = slice(start, start + SEARCH)
-        same = lambda value: value
-
-        def mass(level):
-            wide = jnp.broadcast_to(level, (8, SEARCH))
-            total = column_fold(shifted, place, lambda value: jnp.maximum(value, wide), jnp.add)
-            return jnp.sum(total, axis=0, keepdims=True) - K * level
-
-        high = jnp.max(column_fold(shifted, place, same, jnp.maximum), axis=0, keepdims=True)
-        low = (jnp.sum(column_fold(shifted, place, same, jnp.add), axis=0, keepdims=True) - K) / K
-        mass_low = mass(low)
-        mass_high = jnp.zeros_like(high)
-        for _ in range(BISECT):
-            middle = 0.5 * (low + high)
-            total = mass(middle)
-            above = total > K
-            low = jnp.where(above, middle, low)
-            high = jnp.where(above, high, middle)
-            mass_low = jnp.where(above, total, mass_low)
-            mass_high = jnp.where(above, mass_high, total)
-        levels[:, place] = low + (mass_low - K) * (high - low) / (mass_low - mass_high)
+def find_levels(shifted, place):
+    width = place.stop - place.start
+    same = lambda value: value
+
+    def mass(level):
+        wide = jnp.broadcast_to(level, (8, width))
+        total = column_fold(shifted, place, lambda value: jnp.maximum(value, wide), jnp.add)
+        return jnp.sum(total, axis=0, keepdims=True) - K * level
+
+    high = jnp.max(column_fold(shifted, place, same, jnp.maximum), axis=0, keepdims=True)
+    low = (jnp.sum(column_fold(shifted, place, same, jnp.add), axis=0, keepdims=True) - K) / K
+    mass_low = mass(low)
+    mass_high = jnp.zeros_like(high)
+    for _ in range(BISECT):
+        middle = 0.5 * (low + high)
+        total = mass(middle)
+        above = total > K
+        low = jnp.where(above, middle, low)
+        high = jnp.where(above, high, middle)
+        mass_low = jnp.where(above, total, mass_low)
+        mass_high = jnp.where(above, mass_high, total)
+    return low + (mass_low - K) * (high - low) / (mass_low - mass_high)
+
+
+def update(shifted, place, z_old, u_old, z_new, u_new):
+    width = place.stop - place.start
+    level = jnp.broadcast_to(find_levels(shifted, place), (8, width))
+    primal, change = jnp.zeros((8, width), F32), jnp.zeros((8, width), F32)
+    for k in range(0, K, 8):
+        value = shifted[k:k + 8, place]
+        z, u = jnp.maximum(value - level, 0.0), jnp.minimum(value, level)
+        z_new[k:k + 8, place] = z
+        u_new[k:k + 8, place] = u
+        primal += jnp.square(u - u_old[k:k + 8, place])
+        change += jnp.square(z - z_old[k:k + 8, place])
+    return [sum(value[:, start:start + 128] for start in range(0, width, 128)) for value in (primal, change)]
 
 
 def lane_row(values):
     lane = lax.broadcasted_iota(jnp.int32, (1, 128), 1)
     row = jnp.zeros((1, 128), F32)
-    for place, value in values:
-        row = row + jnp.where(lane == place, jnp.sum(value), 0.0)
+    for place, value in enumerate(values):
+        total = jnp.sum(jnp.sum(value, axis=0, keepdims=True), axis=1, keepdims=True)
+        row = row + jnp.where(lane == place, total, 0.0)
     return row
 
 
 def first_kernel(bands, padded, scale, spectra, endmembers, gram_hbm, z_hbm, u_hbm,
-                 y_out, e_out, m_high, m_low, shifted, levels, sums,
-                 gram, z_ref, u_ref, w_high, w_low, e_send, e_recv, f_send, f_recv, y_send, y_recv, local_sem):
+                 y_out, e_out, m_high, m_low, z_new, u_new, sums,
+                 gram, z_ref, u_ref, shifted, w_high, w_low, e_send, e_recv, f_send, f_recv, y_send, y_recv, local_sem):
     me, pix = lax.axis_index("band"), lax.axis_index("pix")
     core = lax.rem(pix, 2)
     sibling = {"pix": pix + 1 - 2 * core, "band": me}
     rows = spectra.shape[0]
     columns = y_out.shape[1]
-    part = columns // PARTS
+    edges = [columns * edge // 8 for edge in EDGES]
+    parts = list(zip(edges[:-1], edges[1:]))
     half = pl.ds(pl.multiple_of(core * (K // 2), K // 2), K // 2)
 
     def rows_of(band):
@@ -115,10 +130,10 @@
         send_sem=e_send.at[step], recv_sem=e_recv.at[step],
         device_id={"pix": pix, "band": peer}, device_id_type=MESH) for step, peer in enumerate(peers)]
     copies_y = [[pltpu.make_async_remote_copy(
-        src_ref=spectra_of(peer, start, part), dst_ref=y_out.at[rows_of(me), start:start + part],
-        send_sem=y_send.at[start // part, step], recv_sem=y_recv.at[start // part, step],
+        src_ref=spectra_of(peer, start, stop - start), dst_ref=y_out.at[rows_of(me), start:stop],
+        send_sem=y_send.at[index, step], recv_sem=y_recv.at[index, step],
         device_id={"pix": pix, "band": peer}, device_id_type=MESH) for step, peer in enumerate(peers)]
-        for start in range(0, columns, part)]
+        for index, (start, stop) in enumerate(parts)]
     for copy in sum(copies_y, copies_e):
         copy.start()
     copies_f = [pltpu.make_async_remote_copy(
@@ -130,8 +145,8 @@
     for k in range(0, K, 64):
         w_high[k:k + 64, :], w_low[k:k + 64, :] = split(z_ref[k:k + 64, :] - u_ref[k:k + 64, :])
     g_high, g_low = split(gram[...])
-    for start in range(0, columns, part):
-        place = slice(start, start + part)
+    for start in range(0, columns, SEARCH):
+        place = slice(start, start + SEARCH)
         high = w_high[:, place]
         shifted[:, place] = u_ref[:, place] + (mxu(g_high, high) + mxu(g_low, high) + mxu(g_high, w_low[:, place]))
     for arrival, copy in zip(copies_e, copies_f):
@@ -150,21 +165,14 @@
     m_high[...], m_low[...] = split(total * scale)
 
     values = []
-    for index, start in enumerate(range(0, columns, part)):
-        for copy in copies_y[index]:
+    for arrivals, (start, stop) in zip(copies_y, parts):
+        for copy in arrivals:
             copy.wait_recv()
-        place = slice(start, start + part)
+        place = slice(start, stop)
         arrived = y_out[:, place]
         shifted[:, place] += mxu(m_high[...], arrived) + mxu(m_low[...], arrived)
-        find_levels(shifted, levels, start, part)
-        level = jnp.broadcast_to(levels[:, place], (8, part))
-        primal, change = jnp.zeros((8, part), F32), jnp.zeros((8, part), F32)
-        for k in range(0, K, 8):
-            value = shifted[k:k + 8, place]
-            primal += jnp.square(jnp.minimum(value, level) - u_ref[k:k + 8, place])
-            change += jnp.square(jnp.maximum(value - level, 0.0) - z_ref[k:k + 8, place])
-        values += [(0, primal), (2, change)]
-    sums[...] = lane_row(values)
+        values.append(update(shifted, place, z_ref, u_ref, z_new, u_new))
+    sums[0], sums[1] = (sum(pair[which] for pair in values) for which in range(2))
     for copy in sum(copies_y, copies_e + copies_f):
         copy.wait_send()
 
@@ -173,8 +181,8 @@
     return min(step, size - step)
 
 
-def second_kernel(bands, y_ref, e_ref, m_high, m_low, before, levels_before, sums_before, z_out, u_out, totals,
-                  w_high, w_low, shifted, levels, mine, first, middle, second, send1, recv1, send2, recv2):
+def second_kernel(bands, y_ref, e_ref, m_high, m_low, z_old, u_old, sums_before, z_out, u_out, totals,
+                  w_high, w_low, shifted, mine, first, middle, second, send1, recv1, send2, recv2):
     pix, band = lax.axis_index("pix"), lax.axis_index("band")
     core, z, x = lax.rem(pix, 2), lax.rem(pix // 2, LONG), pix // (2 * LONG)
     steps1 = sorted(((dz, dc) for dz in range(LONG) for dc in range(2) if dz or dc),
@@ -189,29 +197,16 @@
     for target in targets2 + targets1:
         pl.semaphore_signal(barrier, inc=1, device_id=target, device_id_type=MESH)
 
-    columns = before.shape[1]
-    level_before = levels_before[...]
+    columns = z_old.shape[1]
     for k in range(0, K, 64):
-        w_high[k:k + 64, :], w_low[k:k + 64, :] = split(jnp.abs(before[k:k + 64, :] - level_before) - level_before)
+        w_high[k:k + 64, :], w_low[k:k + 64, :] = split(z_old[k:k + 64, :] - u_old[k:k + 64, :])
     modelled = (mxu(e_ref[...], w_high[...]) + mxu(e_ref[...], w_low[...])) * (1.0 / K)
     rest = y_ref[...].astype(F32) - modelled
-    shifted[...] = jnp.maximum(before[...] - level_before, 0.0) + apply_model(m_high, m_low, rest)
-    find_levels(shifted, levels, 0, columns)
-    values = []
-    for start in range(0, columns, SEARCH):
-        place = slice(start, start + SEARCH)
-        level = jnp.broadcast_to(levels[:, place], (8, SEARCH))
-        old = jnp.broadcast_to(levels_before[:, place], (8, SEARCH))
-        primal, change = jnp.zeros((8, SEARCH), F32), jnp.zeros((8, SEARCH), F32)
-        for k in range(0, K, 8):
-            value, earlier = shifted[k:k + 8, place], before[k:k + 8, place]
-            z_new, u_new = jnp.maximum(value - level, 0.0), jnp.minimum(value, level)
-            z_out[k:k + 8, place] = z_new
-            u_out[k:k + 8, place] = u_new
-            primal += jnp.square(u_new - jnp.minimum(earlier, old))
-            change += jnp.square(z_new - jnp.maximum(earlier - old, 0.0))
-        values += [(1, primal), (3, change)]
-    row = sums_before[...] + lane_row(values)
+    shifted[...] = z_old[...] + apply_model(m_high, m_low, rest)
+    values = [update(shifted, slice(start, start + SEARCH), z_old, u_old, z_out, u_out)
+              for start in range(0, columns, SEARCH)]
+    primal, change = (sum(pair[which] for pair in values) for which in range(2))
+    row = lane_row([sums_before[0], primal, sums_before[1], change])
     mine[...] = row
     first[0] = row
     pl.semaphore_wait(barrier, len(targets1) + len(targets2))
@@ -258,18 +253,18 @@
     hbm = pl.BlockSpec(memory_space=pltpu.HBM)
     shape = jax.ShapeDtypeStruct
     dma = pltpu.SemaphoreType.DMA
-    square, wide = shape((K, columns), F32), shape((1, columns), F32)
+    square = shape((K, columns), F32)
     line = shape((1, 128), F32)
     big = pltpu.VMEM((K, columns), F32)
     packed = pltpu.VMEM((K, columns), BF16)
-    y, e, m_high, m_low, shifted, levels, sums = pl.pallas_call(
+    y, e, m_high, m_low, z, u, sums = pl.pallas_call(
         functools.partial(first_kernel, bands, padded, 1.0 / (K * penalty)),
         out_shape=(shape((depth, columns), BF16), shape((depth, K), BF16), shape((K, depth), BF16),
-                   shape((K, depth), BF16), square, wide, line),
+                   shape((K, depth), BF16), square, square, shape((2, 8, 128), F32)),
         in_specs=[hbm] * 5,
         out_specs=(vmem,) * 7,
-        scratch_shapes=[pltpu.VMEM((K, K), F32), big, big, packed, packed]
-        + [dma((bands - 1,))] * 4 + [dma((PARTS, bands - 1))] * 2 + [dma((5,))],
+        scratch_shapes=[pltpu.VMEM((K, K), F32), big, big, big, packed, packed]
+        + [dma((bands - 1,))] * 4 + [dma((len(EDGES) - 1, bands - 1))] * 2 + [dma((5,))],
         compiler_params=pltpu.CompilerParams(collective_id=0, has_side_effects=True, vmem_limit_bytes=VMEM_LIMIT),
         name="first",
     )(*[pltpu.with_memory_space_constraint(array, pltpu.HBM)
@@ -281,12 +276,12 @@
         out_shape=(resident, resident, line),
         in_specs=[vmem] * 7,
         out_specs=(vmem,) * 3,
-        scratch_shapes=[packed, packed, big, pltpu.VMEM((1, columns), F32), pltpu.VMEM((1, 128), F32),
+        scratch_shapes=[packed, packed, big, pltpu.VMEM((1, 128), F32),
                         pltpu.VMEM((n1, 1, 128), F32), pltpu.VMEM((1, 128), F32), pltpu.VMEM((n2, 1, 128), F32)]
         + [dma] * 4,
         compiler_params=pltpu.CompilerParams(collective_id=1, has_side_effects=True, vmem_limit_bytes=VMEM_LIMIT),
         name="second",
-    )(y, e, m_high, m_low, shifted, levels, sums)
+    )(y, e, m_high, m_low, z, u, sums)
     return pl.pallas_call(
         functools.partial(last_kernel, pixels),
         out_shape=(square, square, shape((2, 2), F32)),

time: 37.3 us -> 38.1 us (1.021)
  Pallas kernels: 36.6 us -> 37.4 us
    pallas_call x1, Pallas kernels: 15.4 us -> 16.1 us  [body(): pl.pallas_call(functools.partial(first_kernel, bands, padded, 1.0 / (K *...]
where the time goes in v6:
time: 38.1 us
  Pallas kernels  37.4 us (98%)
  between operations  0.65 us (2%)
    pallas_call x1, Pallas kernels, body(): pl.pallas_call(functools.partial(second_kernel, bands), out_shape=(reside...  18.6 us
    pallas_call x1, Pallas kernels, body(): pl.pallas_call(functools.partial(first_kernel, bands, padded, 1.0 / (K *...  16.1 us
    pallas_call x1, Pallas kernels, body(): pl.pallas_call(functools.partial(last_kernel, pixels), out_shape=(square,...  2.63 us

profile of v6, /device:TPU:1, one launch (start us, length us, event | category | flops | bytes accessed | tf_op | source)
XLA Modules:
  0.0 38.1 jit_solution(2840483722219898063)
XLA Ops:
  0.6 16.1 %first.1 = (bf16[256,1024]{1,0:T(8,128)(2,1)S(1)}, bf16[256,512]{1,0:T(8,128)(2,1)S(1)}, bf16[512,256]{1,0:T(8,128)(2,1)S(1)}, bf16[512,256]{1,0:T(8,128)(2,1)S(...) custom-call(bf16[56,4096]{1,0:T(8,128)(2,1)} %spectra.1, ...), custom_call_target="tpu_custom_call" | custom-call | tf_op jit(solution)/shard_map/first/pallas_call | solution.py:260
  16.8 18.6 %second.1 = (f32[512,1024]{1,0:T(8,128)S(1)}, f32[512,1024]{1,0:T(8,128)S(1)}, f32[1,128]{1,0:T(1,128)S(1)}) custom-call(bf16[256,1024]{1,0:T(8,128)(2,1)S(1)} %get-tuple-element.13.y_ref, bf16[256,512]{1,0:T(8,128)(2,1)S(1)} %get-tuple-element.14.e_ref, bf16[512,256]{1,0:T(8,128)(2,1)S(1)} %get-tuple-element.15.m_high, ...), custom_call_target="tpu_custom_call" | custom-call | tf_op jit(solution)/shard_map/second/pallas_call | solution.py:274
  35.4 2.6 %last.1 = (f32[512,1024]{1,0:T(8,128)}, f32[512,1024]{1,0:T(8,128)}, f32[2,2]{1,0:T(2,128)}) custom-call(f32[512,1024]{1,0:T(8,128)S(1)} %get-tuple-element.20.z, f32[512,1024]{1,0:T(8,128)S(1)} %get-tuple-element.21.u, f32[1,128]{1,0:T(1,128)S(1)} %get-tuple-element.22.totals), custom_call_target="tpu_custom_call" | custom-call | tf_op jit(solution)/shard_map/last/pallas_call | solution.py:285

commit v7 on v5

--- a/solution.py
+++ b/solution.py
@@ -70,8 +70,14 @@
     lane = lax.broadcasted_iota(jnp.int32, (1, 128), 1)
     row = jnp.zeros((1, 128), F32)
     for place, value in values:
-        row = row + jnp.where(lane == place, jnp.sum(value), 0.0)
+        row = row + jnp.where(lane == place, jnp.sum(value, axis=1, keepdims=True), 0.0)
     return row
+
+
+def fold_lanes(value):
+    width = value.shape[1]
+    total = sum(value[:, start:start + 128] for start in range(0, width, 128))
+    return jnp.sum(total, axis=0, keepdims=True)
 
 
 def first_kernel(bands, padded, scale, spectra, endmembers, gram_hbm, z_hbm, u_hbm,
@@ -161,9 +167,10 @@
         primal, change = jnp.zeros((8, part), F32), jnp.zeros((8, part), F32)
         for k in range(0, K, 8):
             value = shifted[k:k + 8, place]
-            primal += jnp.square(jnp.minimum(value, level) - u_ref[k:k + 8, place])
-            change += jnp.square(jnp.maximum(value - level, 0.0) - z_ref[k:k + 8, place])
-        values += [(0, primal), (2, change)]
+            dual = jnp.minimum(value, level)
+            primal += jnp.square(dual - u_ref[k:k + 8, place])
+            change += jnp.square(value - dual - z_ref[k:k + 8, place])
+        values += [(0, fold_lanes(primal)), (2, fold_lanes(change))]
     sums[...] = lane_row(values)
     for copy in sum(copies_y, copies_e + copies_f):
         copy.wait_send()
@@ -195,7 +202,7 @@
         w_high[k:k + 64, :], w_low[k:k + 64, :] = split(jnp.abs(before[k:k + 64, :] - level_before) - level_before)
     modelled = (mxu(e_ref[...], w_high[...]) + mxu(e_ref[...], w_low[...])) * (1.0 / K)
     rest = y_ref[...].astype(F32) - modelled
-    shifted[...] = jnp.maximum(before[...] - level_before, 0.0) + apply_model(m_high, m_low, rest)
+    shifted[...] = before[...] - jnp.minimum(before[...], level_before) + apply_model(m_high, m_low, rest)
     find_levels(shifted, levels, 0, columns)
     values = []
     for start in range(0, columns, SEARCH):
@@ -205,12 +212,13 @@
         primal, change = jnp.zeros((8, SEARCH), F32), jnp.zeros((8, SEARCH), F32)
         for k in range(0, K, 8):
             value, earlier = shifted[k:k + 8, place], before[k:k + 8, place]
-            z_new, u_new = jnp.maximum(value - level, 0.0), jnp.minimum(value, level)
+            u_new, u_old = jnp.minimum(value, level), jnp.minimum(earlier, old)
+            z_new = value - u_new
             z_out[k:k + 8, place] = z_new
             u_out[k:k + 8, place] = u_new
-            primal += jnp.square(u_new - jnp.minimum(earlier, old))
-            change += jnp.square(z_new - jnp.maximum(earlier - old, 0.0))
-        values += [(1, primal), (3, change)]
+            primal += jnp.square(u_new - u_old)
+            change += jnp.square(z_new - (earlier - u_old))
+        values += [(1, fold_lanes(primal)), (3, fold_lanes(change))]
     row = sums_before[...] + lane_row(values)
     mine[...] = row
     first[0] = row

time: 37.3 us -> 37.4 us (level)
  no operation moved by 1% of the time
where the time goes in v7:
time: 37.4 us; the launch traced here: 37.3 us
  Pallas kernels  36.7 us (98%)
  between operations  0.65 us (2%)
    pallas_call x1, Pallas kernels, body(): pl.pallas_call(functools.partial(second_kernel, bands), out_shape=(reside...  18.6 us
    pallas_call x1, Pallas kernels, body(): pl.pallas_call(functools.partial(first_kernel, bands, padded, 1.0 / (K *...  15.4 us
    pallas_call x1, Pallas kernels, body(): pl.pallas_call(functools.partial(last_kernel, pixels), out_shape=(square,...  2.63 us

profile of v7, /device:TPU:1, one launch (start us, length us, event | category | flops | bytes accessed | tf_op | source)
XLA Modules:
  0.0 37.3 jit_solution(18272322001529543068)
XLA Ops:
  0.6 15.4 %first.1 = (bf16[256,1024]{1,0:T(8,128)(2,1)S(1)}, bf16[256,512]{1,0:T(8,128)(2,1)S(1)}, bf16[512,256]{1,0:T(8,128)(2,1)S(1)}, bf16[512,256]{1,0:T(8,128)(2,1)S(...) custom-call(bf16[56,4096]{1,0:T(8,128)(2,1)} %spectra.1, bf16[56,512]{1,0:T(8,128)(2,1)} %endmembers.1, ...), custom_call_target="tpu_custom_call" | custom-call | tf_op jit(solution)/shard_map/first/pallas_call | solution.py:273
  16.1 18.6 %second.1 = (f32[512,1024]{1,0:T(8,128)S(1)}, f32[512,1024]{1,0:T(8,128)S(1)}, f32[1,128]{1,0:T(1,128)S(1)}) custom-call(bf16[256,1024]{1,0:T(8,128)(2,1)S(1)} %get-tuple-element.13.y_ref, bf16[256,512]{1,0:T(8,128)(2,1)S(1)} %get-tuple-element.14.e_ref, bf16[512,256]{1,0:T(8,128)(2,1)S(1)} %get-tuple-element.15.m_high, ...), custom_call_target="tpu_custom_call" | custom-call | tf_op jit(solution)/shard_map/second/pallas_call | solution.py:287
  34.7 2.6 %last.1 = (f32[512,1024]{1,0:T(8,128)}, f32[512,1024]{1,0:T(8,128)}, f32[2,2]{1,0:T(2,128)}) custom-call(f32[512,1024]{1,0:T(8,128)S(1)} %get-tuple-element.20.z, f32[512,1024]{1,0:T(8,128)S(1)} %get-tuple-element.21.u, f32[1,128]{1,0:T(1,128)S(1)} %get-tuple-element.22.totals), custom_call_target="tpu_custom_call" | custom-call | tf_op jit(solution)/shard_map/last/pallas_call | solution.py:298

commit v8 on v5

--- a/solution.py
+++ b/solution.py
@@ -33,36 +33,36 @@
     return mxu(m_high[...], high) + mxu(m_low[...], high) + mxu(m_high[...], low)
 
 
-def column_fold(ref, place, change, fold):
-    total = None
-    for k in range(0, K, 8):
-        value = change(ref[k:k + 8, place])
-        total = value if total is None else fold(total, value)
-    return total
-
-
 def find_levels(shifted, levels, begin, width):
     for start in range(begin, begin + width, SEARCH):
         place = slice(start, start + SEARCH)
-        same = lambda value: value
-
-        def mass(level):
-            wide = jnp.broadcast_to(level, (8, SEARCH))
-            total = column_fold(shifted, place, lambda value: jnp.maximum(value, wide), jnp.add)
-            return jnp.sum(total, axis=0, keepdims=True) - K * level
-
-        high = jnp.max(column_fold(shifted, place, same, jnp.maximum), axis=0, keepdims=True)
-        low = (jnp.sum(column_fold(shifted, place, same, jnp.add), axis=0, keepdims=True) - K) / K
-        mass_low = mass(low)
+
+        def masses(*candidates):
+            wide = [jnp.broadcast_to(level, (8, SEARCH)) for level in candidates]
+            totals = [jnp.zeros((8, SEARCH), F32) for _ in wide]
+            for k in range(0, K, 8):
+                value = shifted[k:k + 8, place]
+                totals = [total + jnp.maximum(value, level) for total, level in zip(totals, wide)]
+            return [jnp.sum(total, axis=0, keepdims=True) - K * level for total, level in zip(totals, candidates)]
+
+        high = total = shifted[0:8, place]
+        for k in range(8, K, 8):
+            value = shifted[k:k + 8, place]
+            high, total = jnp.maximum(high, value), total + value
+        high = jnp.max(high, axis=0, keepdims=True)
+        low = (jnp.sum(total, axis=0, keepdims=True) - K) / K
+        middle = 0.5 * (low + high)
+        mass_low, total = masses(low, middle)
         mass_high = jnp.zeros_like(high)
-        for _ in range(BISECT):
-            middle = 0.5 * (low + high)
-            total = mass(middle)
+        for step in range(BISECT):
             above = total > K
             low = jnp.where(above, middle, low)
             high = jnp.where(above, high, middle)
             mass_low = jnp.where(above, total, mass_low)
             mass_high = jnp.where(above, mass_high, total)
+            if step < BISECT - 1:
+                middle = 0.5 * (low + high)
+                total, = masses(middle)
         levels[:, place] = low + (mass_low - K) * (high - low) / (mass_low - mass_high)
 
 

time: 37.3 us -> 37.1 us (level)
  no operation moved by 1% of the time
where the time goes in v8:
time: 37.1 us; the launch traced here: 37 us
  Pallas kernels  36.4 us (98%)
  between operations  0.65 us (2%)
    pallas_call x1, Pallas kernels, body(): pl.pallas_call(functools.partial(second_kernel, bands), out_shape=(reside...  18.5 us
    pallas_call x1, Pallas kernels, body(): pl.pallas_call(functools.partial(first_kernel, bands, padded, 1.0 / (K *...  15.3 us
    pallas_call x1, Pallas kernels, body(): pl.pallas_call(functools.partial(last_kernel, pixels), out_shape=(square,...  2.63 us

profile of v8, /device:TPU:1, one launch (start us, length us, event | category | flops | bytes accessed | tf_op | source)
XLA Modules:
  0.0 37.0 jit_solution(5697368413409823291)
XLA Ops:
  0.6 15.3 %first.1 = (bf16[256,1024]{1,0:T(8,128)(2,1)S(1)}, bf16[256,512]{1,0:T(8,128)(2,1)S(1)}, bf16[512,256]{1,0:T(8,128)(2,1)S(1)}, bf16[512,256]{1,0:T(8,128)(2,1)S(...) custom-call(bf16[56,4096]{1,0:T(8,128)(2,1)} %spectra.1, bf16[56,512]{1,0:T(8,128)(2,1)} %endmembers.1, ...), custom_call_target="tpu_custom_call" | custom-call | tf_op jit(solution)/shard_map/first/pallas_call | solution.py:265
  15.9 18.5 %second.1 = (f32[512,1024]{1,0:T(8,128)S(1)}, f32[512,1024]{1,0:T(8,128)S(1)}, f32[1,128]{1,0:T(1,128)S(1)}) custom-call(bf16[256,1024]{1,0:T(8,128)(2,1)S(1)} %get-tuple-element.13.y_ref, bf16[256,512]{1,0:T(8,128)(2,1)S(1)} %get-tuple-element.14.e_ref, bf16[512,256]{1,0:T(8,128)(2,1)S(1)} %get-tuple-element.15.m_high, ...), custom_call_target="tpu_custom_call" | custom-call | tf_op jit(solution)/shard_map/second/pallas_call | solution.py:279
  34.4 2.6 %last.1 = (f32[512,1024]{1,0:T(8,128)}, f32[512,1024]{1,0:T(8,128)}, f32[2,2]{1,0:T(2,128)}) custom-call(f32[512,1024]{1,0:T(8,128)S(1)} %get-tuple-element.20.z, f32[512,1024]{1,0:T(8,128)S(1)} %get-tuple-element.21.u, f32[1,128]{1,0:T(1,128)S(1)} %get-tuple-element.22.totals), custom_call_target="tpu_custom_call" | custom-call | tf_op jit(solution)/shard_map/last/pallas_call | solution.py:290

commit v9 on v8

--- a/solution.py
+++ b/solution.py
@@ -34,35 +34,36 @@
 
 
 def find_levels(shifted, levels, begin, width):
-    for start in range(begin, begin + width, SEARCH):
-        place = slice(start, start + SEARCH)
-
-        def masses(*candidates):
-            wide = [jnp.broadcast_to(level, (8, SEARCH)) for level in candidates]
-            totals = [jnp.zeros((8, SEARCH), F32) for _ in wide]
-            for k in range(0, K, 8):
-                value = shifted[k:k + 8, place]
-                totals = [total + jnp.maximum(value, level) for total, level in zip(totals, wide)]
-            return [jnp.sum(total, axis=0, keepdims=True) - K * level for total, level in zip(totals, candidates)]
-
+    places = [slice(start, start + SEARCH) for start in range(begin, begin + width, SEARCH)]
+
+    def masses(place, *candidates):
+        wide = [jnp.broadcast_to(level, (8, SEARCH)) for level in candidates]
+        totals = [jnp.zeros((8, SEARCH), F32) for _ in wide]
+        for k in range(0, K, 8):
+            value = shifted[k:k + 8, place]
+            totals = [total + jnp.maximum(value, level) for total, level in zip(totals, wide)]
+        return [jnp.sum(total, axis=0, keepdims=True) - K * level for total, level in zip(totals, candidates)]
+
+    states = []
+    for place in places:
         high = total = shifted[0:8, place]
         for k in range(8, K, 8):
             value = shifted[k:k + 8, place]
             high, total = jnp.maximum(high, value), total + value
         high = jnp.max(high, axis=0, keepdims=True)
         low = (jnp.sum(total, axis=0, keepdims=True) - K) / K
-        middle = 0.5 * (low + high)
-        mass_low, total = masses(low, middle)
-        mass_high = jnp.zeros_like(high)
-        for step in range(BISECT):
+        states.append((low, high, None, jnp.zeros_like(high)))
+    for step in range(BISECT):
+        for index, (place, (low, high, mass_low, mass_high)) in enumerate(zip(places, states)):
+            middle = 0.5 * (low + high)
+            if step == 0:
+                mass_low, total = masses(place, low, middle)
+            else:
+                total, = masses(place, middle)
             above = total > K
-            low = jnp.where(above, middle, low)
-            high = jnp.where(above, high, middle)
-            mass_low = jnp.where(above, total, mass_low)
-            mass_high = jnp.where(above, mass_high, total)
-            if step < BISECT - 1:
-                middle = 0.5 * (low + high)
-                total, = masses(middle)
+            states[index] = (jnp.where(above, middle, low), jnp.where(above, high, middle),
+                             jnp.where(above, total, mass_low), jnp.where(above, mass_high, total))
+    for place, (low, high, mass_low, mass_high) in zip(places, states):
         levels[:, place] = low + (mass_low - K) * (high - low) / (mass_low - mass_high)
 
 

time: 37.1 us -> 37.1 us (level)
  no operation moved by 1% of the time
where the time goes in v9:
time: 37.1 us; the launch traced here: 37 us
  Pallas kernels  36.4 us (98%)
  between operations  0.65 us (2%)
    pallas_call x1, Pallas kernels, body(): pl.pallas_call(functools.partial(second_kernel, bands), out_shape=(reside...  18.5 us
    pallas_call x1, Pallas kernels, body(): pl.pallas_call(functools.partial(first_kernel, bands, padded, 1.0 / (K *...  15.3 us
    pallas_call x1, Pallas kernels, body(): pl.pallas_call(functools.partial(last_kernel, pixels), out_shape=(square,...  2.63 us

profile of v9, /device:TPU:1, one launch (start us, length us, event | category | flops | bytes accessed | tf_op | source)
XLA Modules:
  0.0 37.0 jit_solution(5697368413409823291)
XLA Ops:
  0.6 15.3 %first.1 = (bf16[256,1024]{1,0:T(8,128)(2,1)S(1)}, bf16[256,512]{1,0:T(8,128)(2,1)S(1)}, bf16[512,256]{1,0:T(8,128)(2,1)S(1)}, bf16[512,256]{1,0:T(8,128)(2,1)S(...) custom-call(bf16[56,4096]{1,0:T(8,128)(2,1)} %spectra.1, bf16[56,512]{1,0:T(8,128)(2,1)} %endmembers.1, ...), custom_call_target="tpu_custom_call" | custom-call | tf_op jit(solution)/shard_map/first/pallas_call | solution.py:266
  15.9 18.5 %second.1 = (f32[512,1024]{1,0:T(8,128)S(1)}, f32[512,1024]{1,0:T(8,128)S(1)}, f32[1,128]{1,0:T(1,128)S(1)}) custom-call(bf16[256,1024]{1,0:T(8,128)(2,1)S(1)} %get-tuple-element.13.y_ref, bf16[256,512]{1,0:T(8,128)(2,1)S(1)} %get-tuple-element.14.e_ref, bf16[512,256]{1,0:T(8,128)(2,1)S(1)} %get-tuple-element.15.m_high, ...), custom_call_target="tpu_custom_call" | custom-call | tf_op jit(solution)/shard_map/second/pallas_call | solution.py:280
  34.4 2.6 %last.1 = (f32[512,1024]{1,0:T(8,128)}, f32[512,1024]{1,0:T(8,128)}, f32[2,2]{1,0:T(2,128)}) custom-call(f32[512,1024]{1,0:T(8,128)S(1)} %get-tuple-element.20.z, f32[512,1024]{1,0:T(8,128)S(1)} %get-tuple-element.21.u, f32[1,128]{1,0:T(1,128)S(1)} %get-tuple-element.22.totals), custom_call_target="tpu_custom_call" | custom-call | tf_op jit(solution)/shard_map/last/pallas_call | solution.py:291
